TPU v7x, 256 devices: a whole 4x4x8 slice. The times are simulated.
256 devices in a mesh: tile: 16 (over y, z_hi), head: 16 (over x, z_lo, core).
Axes of the slice: x: 4, y: 4, z: 8 (z_hi: 4, z_lo: 2; z = z_hi * 2 + z_lo), core: 2. Of those that a mesh axis runs over, the one named last changes fastest.
Arguments:
- tokens: bfloat16 [6144, 3072], P('tile'), may hold values from -200 to 200
- mod_shift: float32 [3072], replicated, may hold values from -3 to 3
- mod_scale: float32 [3072], replicated, may hold values from -2.5 to 2.5
- mod_gate: float32 [3072], replicated, may hold values from -4 to 4
- qkv_weight: bfloat16 [3072, 6144], P(None, 'head'), may hold values from -1 to 1
- out_weight: bfloat16 [2048, 3072], P('head'), may hold values from -0.125 to 0.125
- teacher: bfloat16 [6144, 3072], P('tile'), may hold values from -6 to 6
- slot_tiles: int32 [16], replicated, may hold values from 0 to 15, each once
Outputs:
- qkv_grad: float32 [3072, 6144], P('tile', 'head')
- out_grad: float32 [2048, 3072], P('head', 'tile')
Inputs may be any that keep to these rules, and one draw needn't show every extreme that they name: Slot s, rows s * 384 to (s + 1) * 384 - 1 of tokens and teacher, holds tile slot_tiles[s]; every tile once.
All inputs are finite; a program needn't handle non-finite values.
Results may differ from a plain program's by a relative error of at most 0.00049.
Values may be sent and summed in bfloat16 or wider, within the bound.
A program may use at most 128 MiB of HBM per device.

v0:
```python
import math

import jax
import jax.numpy as jnp
from jax import lax
from jax.sharding import PartitionSpec as P

HD = 128
TOK_TILE = 384
TT = 1
TH = 4


EPS_NORM = 1e-05
EPS_ROOT = 1e-06
LOSS_WEIGHT = 32.0


def modulated_norm(tokens, mod_shift, mod_scale):
    values_in = tokens.astype(jnp.float32)
    center = values_in - jnp.mean(values_in, -1, keepdims=True)
    spread = jnp.mean(center * center, -1, keepdims=True)
    return (center * lax.rsqrt(spread + EPS_NORM) * (1.0 + mod_scale) + mod_shift).astype(
        jnp.bfloat16
    )


def root_norm(values):
    factor = lax.rsqrt(jnp.mean(values * values, -1, keepdims=True) + EPS_ROOT)
    return (values * factor, factor)


def root_norm_back(grad_unit, unit_value, factor):
    return factor * (grad_unit - unit_value * jnp.mean(grad_unit * unit_value, -1, keepdims=True))


def tiles_of(slot_tiles, slot_ids):
    onehot = (
        slot_ids[:, None] == jnp.arange(slot_tiles.shape[0], dtype=jnp.int32)[None, :]
    ).astype(jnp.int32)
    return jnp.sum(onehot * slot_tiles[None, :], 1)


def near_tiles(first_tiles, second_tiles, width_tiles):

    def coords(ids):
        return (ids // (TH * width_tiles), ids // width_tiles % TH, ids % width_tiles)

    ta, ha, wa = coords(first_tiles[:, None])
    tb, hb, wb = coords(second_tiles[None, :])
    close = (jnp.abs(ta - tb) <= 1) & (jnp.abs(ha - hb) <= 1) & (jnp.abs(wa - wb) <= 1)
    return close.astype(jnp.float32)


def masked_exp(queries, keys, tile_mask, group_rows):
    att_scale = 1.0 / math.sqrt(HD)
    scores = (
        jnp.einsum("qhd,khd->hqk", queries, keys, preferred_element_type=jnp.float32) * att_scale
    )
    head_count, query_count, key_count = scores.shape
    shaped = jnp.exp(scores).reshape(
        head_count, query_count // group_rows, group_rows, key_count // TOK_TILE, TOK_TILE
    )
    shaped = shaped * tile_mask[None, :, None, :, None]
    return shaped.reshape(head_count, query_count, key_count)


def per_device(tokens, mod_shift, mod_scale, mod_gate, qkv_weight, out_weight, teacher, slot_tiles):
    tok_rows = tokens.shape[0]
    local_tiles = tok_rows // TOK_TILE
    head_count = out_weight.shape[0] // HD
    width_tiles = slot_tiles.shape[0] // (TT * TH)
    att_scale = 1.0 / math.sqrt(HD)
    normed = modulated_norm(tokens, mod_shift, mod_scale)
    projected = jnp.dot(normed, qkv_weight, preferred_element_type=jnp.float32).reshape(
        tok_rows, head_count, 3, HD
    )
    query_unit, query_factor = root_norm(projected[:, :, 0])
    key_unit, key_factor = root_norm(projected[:, :, 1])
    query_b = query_unit.astype(jnp.bfloat16)
    key_b = key_unit.astype(jnp.bfloat16)
    value_b = projected[:, :, 2].astype(jnp.bfloat16)
    all_keys, all_values = (
        lax.all_gather(key_b, "tile", axis=0, tiled=True),
        lax.all_gather(value_b, "tile", axis=0, tiled=True),
    )
    my_slots = lax.axis_index("tile") * local_tiles + jnp.arange(local_tiles, dtype=jnp.int32)
    my_tiles = tiles_of(slot_tiles, my_slots)
    tile_mask = near_tiles(my_tiles, slot_tiles, width_tiles)
    exp_scores = masked_exp(query_b, all_keys, tile_mask, TOK_TILE)
    totals = jnp.sum(exp_scores, -1)
    att_probs = exp_scores / totals[:, :, None]
    probs_b = att_probs.astype(jnp.bfloat16)
    attended = jnp.einsum(
        "hqk,khd->qhd", probs_b, all_values, preferred_element_type=jnp.float32
    ).astype(jnp.bfloat16)
    flat_att = attended.reshape(tok_rows, head_count * HD)
    partial_branch = jnp.dot(flat_att, out_weight, preferred_element_type=jnp.float32)
    whole_branch = lax.psum(partial_branch, "head")
    residual = LOSS_WEIGHT * (mod_gate * whole_branch - teacher.astype(jnp.float32))
    grad_branch = (mod_gate * residual).astype(jnp.bfloat16)
    contract_rows = (((0,), (0,)), ((), ()))
    out_term = lax.dot_general(
        flat_att, grad_branch, contract_rows, preferred_element_type=jnp.float32
    )
    grad_att = lax.dot_general(
        grad_branch, out_weight, (((1,), (1,)), ((), ())), preferred_element_type=jnp.float32
    )
    grad_att = grad_att.reshape(tok_rows, head_count, HD).astype(jnp.bfloat16)
    row_delta = jnp.sum(grad_att.astype(jnp.float32) * attended.astype(jnp.float32), -1)
    grad_probs = jnp.einsum(
        "qhd,khd->hqk", grad_att, all_values, preferred_element_type=jnp.float32
    )
    grad_scores = (att_probs * (grad_probs - row_delta.T[:, :, None])).astype(jnp.bfloat16)
    grad_query_unit = (
        jnp.einsum("hqk,khd->qhd", grad_scores, all_keys, preferred_element_type=jnp.float32)
        * att_scale
    )
    key_terms = (
        jnp.einsum("hqk,qhd->khd", grad_scores, query_b, preferred_element_type=jnp.float32)
        * att_scale
    )
    value_terms = jnp.einsum("hqk,qhd->khd", probs_b, grad_att, preferred_element_type=jnp.float32)
    grad_key_unit, grad_value = (
        lax.psum_scatter(key_terms, "tile", scatter_dimension=0, tiled=True),
        lax.psum_scatter(value_terms, "tile", scatter_dimension=0, tiled=True),
    )
    grad_query = root_norm_back(grad_query_unit, query_unit, query_factor)
    grad_key = root_norm_back(grad_key_unit, key_unit, key_factor)
    grad_qkv = (
        jnp.stack([grad_query, grad_key, grad_value], 2)
        .astype(jnp.bfloat16)
        .reshape(tok_rows, head_count * 3 * HD)
    )
    qkv_term = lax.dot_general(normed, grad_qkv, contract_rows, preferred_element_type=jnp.float32)
    qkv_grad, out_grad = (
        lax.psum_scatter(qkv_term, "tile", scatter_dimension=0, tiled=True),
        lax.psum_scatter(out_term, "tile", scatter_dimension=1, tiled=True),
    )
    return (qkv_grad, out_grad)


def solution(mesh):
    return jax.shard_map(
        per_device,
        mesh=mesh,
        in_specs=(
            P("tile", None),
            P(),
            P(),
            P(),
            P(None, "head"),
            P("head", None),
            P("tile", None),
            P(),
        ),
        out_specs=(P("tile", "head"), P("head", "tile")),
        check_vma=False,
    )
```

profile of v0, /device:TPU:4, one launch (start us, length us, event | category | flops | bytes accessed | tf_op | source)
XLA Modules:
  0.0 681.5 jit_solution(16059884396941234523)
XLA Ops:
  7.2 0.0 copy-start
  7.2 0.0 all-gather.4.cloned.1.call-start
  7.2 0.0 copy-start.2
  7.3 2.2 convert_reduce_fusion
  9.5 2.4 fusion.3
  12.0 0.0 copy-start.9
  12.0 1.7 fusion.47
  13.7 0.7 fusion.29
  14.4 0.0 all-gather.4.cloned.1.call-update
  14.4 0.0 all-gather.6.cloned.1.call-start
  14.4 0.7 slice.40
  15.1 0.0 all-gather.6.cloned.1.call-update
  15.1 0.0 all-reduce.2.cloned.1.call-start
  15.2 0.7 fusion.39
  18.7 0.1 mul.242
  18.8 56.9 %all-gather.4.cloned.1.call-done = bf16[6144,1,128]{0,2,1:T(8,128)(2,1)} async-done(((bf16[384,1,128]{0,2,1:T(8,128)(2,1)}), bf16[6144,1,128]{0,2,1:T(8,128)(2,1)}) %all-gather.4.cloned.1.call-update) | async-done | bytes 1572880 | tf_op jit(solution)/shard_map/all_gather | solution.py:84
  75.7 7.2 %fusion.49 = (f32[384]{0:T(512)S(1)}, f32[384,6144]{1,0:T(8,128)}) fusion(f32[6144]{0:T(1024)S(1)} %mul.243, bf16[6144,1,128]{0,2,1:T(8,128)(2,1)} %all-gather.4.cloned.1.call-done, f32[384,1,3,128]{0,3,2,1:T(8,128)S(1)} %bitcast.101, f32[384]{0:T(512)S(1)} %add_rsqrt_fusion.1), kind=kOutput, calls=%fused_computation.80 | convolution fusion | flops 611155584 | bytes 11234816 | tf_op jit(solution)/shard_map/qhd,khd->hqk/dot_general | solution.py:58
  83.0 52.0 %all-gather.6.cloned.1.call-done = bf16[6144,1,1,128]{0,3,2,1:T(8,128)(2,1)} async-done(((bf16[384,1,1,128]{0,3,2,1:T(8,128)(2,1)}), bf16[6144,1,1,128]{0,3,2,1:T(8,128)(2,1)}) %all-gather.6.cloned.1.call-update) | async-done | bytes 1572880 | tf_op jit(solution)/shard_map/all_gather | solution.py:85
  134.9 5.8 fusion.21
  140.8 0.0 copy-done.4
  140.8 0.0 copy-start.7
  140.8 2.9 fusion.35
  143.7 0.0 all-reduce.2.cloned.1.call-update
  143.7 0.0 reduce-scatter.5.cloned.1.call-start
  143.8 132.5 %all-reduce.2.cloned.1.call-done = f32[384,3072]{1,0:T(8,128)} async-done(((f32[384,3072]{1,0:T(8,128)}), f32[384,3072]{1,0:T(8,128)}) %all-reduce.2.cloned.1.call-update) | async-done | bytes 4718608 | tf_op jit(solution)/shard_map/psum | solution.py:99
  276.3 4.0 multiply_convert_fusion.1
  280.3 0.8 fusion.26
  281.2 0.6 copy-done.3
  281.7 4.6 multiply_convert_fusion
  286.4 2.2 copy-done.1
  288.6 2.6 fusion
  291.2 0.0 reduce-scatter.5.cloned.1.call-update
  291.3 0.0 reduce-scatter.7.cloned.1.call-start
  291.3 6.4 convolution_bitcast_fusion
  297.7 0.0 reduce-scatter.7.cloned.1.call-update
  297.7 0.2 reduce-scatter.11.cloned.1.call-start
  298.0 3.9 fusion.33
  301.8 0.0 reduce-scatter.11.cloned.1.call-update
  301.9 0.0 reduce-scatter.9.cloned.1.call-start
  301.9 88.6 %reduce-scatter.5.cloned.1.call-done = f32[384,1,128]{0,2,1:T(8,128)} async-done(((f32[6144,1,128]{0,2,1:T(8,128)}), f32[384,1,128]{0,2,1:T(8,128)}) %reduce-scatter.5.cloned.1.call-update) | async-done | bytes 196624 | tf_op jit(solution)/shard_map/reduce_scatter | solution.py:125
  390.5 4.4 multiply_reduce_fusion.1
  394.9 88.5 %reduce-scatter.7.cloned.1.call-done = f32[384,1,128]{0,2,1:T(8,128)} async-done(((f32[6144,1,128]{0,2,1:T(8,128)}), f32[384,1,128]{0,2,1:T(8,128)}) %reduce-scatter.7.cloned.1.call-update) | async-done | bytes 196624 | tf_op jit(solution)/shard_map/reduce_scatter | solution.py:126
  483.4 0.9 convert_bitcast_fusion
  484.3 0.1 fusion.31
  484.4 5.6 fusion.45
  490.0 0.0 reduce-scatter.9.cloned.1.call-update
  490.0 82.3 %reduce-scatter.11.cloned.1.call-done = f32[128,192]{0,1:T(8,128)} async-done(((f32[128,3072]{0,1:T(8,128)}), f32[128,192]{0,1:T(8,128)}) %reduce-scatter.11.cloned.1.call-update) | async-done | bytes 98320 | tf_op jit(solution)/shard_map/reduce_scatter | solution.py:138
  572.3 102.3 %reduce-scatter.9.cloned.1.call-done = f32[192,384]{1,0:T(8,128)} async-done(((f32[3072,384]{1,0:T(8,128)}), f32[192,384]{1,0:T(8,128)}) %reduce-scatter.9.cloned.1.call-update) | async-done | bytes 294928 | tf_op jit(solution)/shard_map/reduce_scatter | solution.py:137
  (28 shorter events, 0.2 us)
Async XLA Ops:
  7.2 4.8 copy-start
  7.2 4.7 copy-start.8
  7.2 4.7 copy-start.11
  7.2 68.5 %all-gather.4.cloned.1.call-start = ((), (), s32[]{:S(2)}) async-start(), calls=%async_computation.4 | async-start | bytes 1671168 | tf_op jit(solution)/shard_map/all_gather | solution.py:84
  7.2 4.7 copy-start.2
  12.0 3.2 copy-start.9
  14.4 120.6 %all-gather.6.cloned.1.call-start = ((), (), s32[]{:S(2)}) async-start(), calls=%async_computation.10 | async-start | bytes 1671168 | tf_op jit(solution)/shard_map/all_gather | solution.py:85
  15.1 261.2 %all-reduce.2.cloned.1.call-start = ((), (), s32[]{:S(2)}) async-start(), calls=%async_computation.5 | async-start | bytes 9437184 | tf_op jit(solution)/shard_map/psum | solution.py:99
  134.9 5.8 copy-start.4
  140.8 3.0 copy-start.7
  143.7 246.7 %reduce-scatter.5.cloned.1.call-start = ((), (), s32[]{:S(2)}) async-start(), calls=%async_computation.6 | async-start | bytes 3342336 | tf_op jit(solution)/shard_map/reduce_scatter | solution.py:125
  276.3 4.0 copy-start.5
  276.3 5.4 copy-start.10
  280.3 1.4 copy-start.3
  286.4 2.2 copy-start.1
  291.3 192.1 %reduce-scatter.7.cloned.1.call-start = ((), (), s32[]{:S(2)}) async-start(), calls=%async_computation.7 | async-start | bytes 3342336 | tf_op jit(solution)/shard_map/reduce_scatter | solution.py:126
  297.7 274.6 %reduce-scatter.11.cloned.1.call-start = ((), (), s32[]{:S(2)}) async-start(), calls=%async_computation.9 | async-start | bytes 1671168 | tf_op jit(solution)/shard_map/reduce_scatter | solution.py:138
  301.9 372.8 %reduce-scatter.9.cloned.1.call-start = ((), (), s32[]{:S(2)}) async-start(), calls=%async_computation.8 | async-start | bytes 5013504 | tf_op jit(solution)/shard_map/reduce_scatter | solution.py:137
  390.5 93.8 %copy-start.6 = (f32[384,1,128]{0,2,1:T(8,128)S(1)}, f32[384,1,128]{0,2,1:T(8,128)}, u32[]{:S(2)}) copy-start(f32[384,1,128]{0,2,1:T(8,128)} %reduce-scatter.5.cloned.1.call-done) | copy-start | bytes 589828
Sparse Core Ops, SparseCore 0:
  14.5 61.1 all-gather.3
  78.7 56.1 all-gather.5
  143.9 132.3 all-reduce.1
  291.4 99.0 reduce-scatter.4
  393.9 89.3 reduce-scatter.6
  487.3 84.9 reduce-scatter.10
  576.5 98.0 reduce-scatter.8
where the time goes:
time: 682 us; the launch traced here: 681 us
  waiting for transfers between devices  603 us (88%)
  matrix products  46 us (7%)
  between operations  17.2 us (3%)
  other arithmetic  11.1 us (2%)
    psum x1, waiting for transfers between devices, per_device(): whole_branch = lax.psum(partial_branch, 'head')  132 us
    reduce_scatter x1, waiting for transfers between devices, per_device(): lax.psum_scatter(qkv_term, 'tile', scatter_dimension=0, tiled=True)  102 us
    reduce_scatter x1, waiting for transfers between devices, per_device(): lax.psum_scatter(key_terms, 'tile', scatter_dimension=0, tiled=True)  88.6 us
    reduce_scatter x1, waiting for transfers between devices, per_device(): lax.psum_scatter(value_terms, 'tile', scatter_dimension=0, tiled=True)  88.5 us
    reduce_scatter x1, waiting for transfers between devices, per_device(): lax.psum_scatter(out_term, 'tile', scatter_dimension=1, tiled=True)  82.3 us
    all_gather x1, waiting for transfers between devices, per_device(): lax.all_gather(key_b, 'tile', axis=0, tiled=True)  56.9 us
    all_gather x1, waiting for transfers between devices, per_device(): lax.all_gather(value_b, 'tile', axis=0, tiled=True)  52 us
  transfers between devices with their start and end apart: 7, of which 7 were waited for; matrix products, arithmetic and copies ran while one was open for 4% of the time, Pallas kernels for 0%

commit v1 on v0

v1 whole, which is shorter than its diff:
```python
import functools
import math

import jax
import jax.numpy as jnp
from jax import lax
from jax.experimental import pallas as pl
from jax.experimental.pallas import tpu as pltpu
from jax.sharding import PartitionSpec as P

HD = 128
TOK_TILE = 384
TH = 4
TW = 4
SIDE = 4
EPS_NORM = 1e-05
EPS_ROOT = 1e-06
LOSS_WEIGHT = 32.0
ATT_SCALE = 1.0 / math.sqrt(HD)
BF16 = jnp.bfloat16
F32 = jnp.float32
MESH = pl.DeviceIdType.MESH
NT = (((1,), (1,)), ((), ()))
VMEM_LIMIT = 60 * 1024 * 1024


class Places:

    def __init__(self):
        self.t = lax.axis_index("tile")
        self.h = lax.axis_index("head")
        self.a = self.t // SIDE
        self.b = self.t % SIDE
        self.x = self.h // 4
        self.lo = self.h % 4

    def tile(self, j, k):
        return lax.rem(self.a + j, SIDE) * SIDE + lax.rem(self.b + k, SIDE)

    def head(self, j, flip):
        lo = self.lo
        if flip & 1:
            lo = lo + 1 - 2 * lax.rem(lo, 2)
        if flip & 2:
            lo = lax.rem(lo + 2, 4)
        return lax.rem(self.x + j, 4) * 4 + lo


TASK_SEMS = {"tag": 16, "hag": 16, "ha2a": 16, "ycols": 4, "yag": 4, "ya2a": 4, "za2a": 4}


def task_peers(kind):
    if kind == "tag":
        return {("t", 0, k) for k in (1, 2, 3)} | {("t", j, 0) for j in (1, 2, 3)}
    if kind == "hag":
        return {("h", j, 0) for j in (1, 2, 3)} | {("h", 0, 2), ("h", 0, 1)}
    if kind == "ha2a":
        return {("h", j, f) for j in range(4) for f in range(4)} - {("h", 0, 0)}
    if kind == "za2a":
        return {("t", 0, k) for k in (1, 2, 3)}
    return {("t", j, 0) for j in (1, 2, 3)}


def out_slots(kind):
    return 16 if kind in ("tag", "hag", "ha2a") else 4


def comm_kernel(kinds, *refs):
    n = len(kinds)
    ins, outs = refs[:n], refs[n : 2 * n]
    sems = refs[2 * n :]
    at = Places()

    def device(peer):
        axis, j, k = peer
        if axis == "t":
            return (at.tile(j, k), at.h)
        return (at.t, at.head(j, k))

    def back(peer):
        axis, j, k = peer
        if axis == "t":
            return ("t", (4 - j) % 4, (4 - k) % 4)
        return ("h", (4 - j) % 4, k)

    peers = sorted(set().union(*[task_peers(kind) for kind in kinds]))
    barrier = pltpu.get_barrier_semaphore()
    for peer in peers:
        pl.semaphore_signal(barrier, inc=1, device_id=device(peer), device_id_type=MESH)
    pl.semaphore_wait(barrier, len(peers))

    started = []
    locals_ = []

    def send(i, src, slot, index, peer):
        copy = pltpu.make_async_remote_copy(
            src_ref=src,
            dst_ref=outs[i].at[slot],
            send_sem=sems[3 * i].at[index],
            recv_sem=sems[3 * i + 1].at[index],
            device_id=device(peer),
            device_id_type=MESH,
        )
        copy.start()
        started.append(copy)

    def arrive(i, slot, index, peer):
        pltpu.make_async_remote_copy(
            src_ref=outs[i].at[slot],
            dst_ref=outs[i].at[slot],
            send_sem=sems[3 * i].at[index],
            recv_sem=sems[3 * i + 1].at[index],
            device_id=device(peer),
            device_id_type=MESH,
        ).wait_recv()

    def keep(i, src, slot):
        copy = pltpu.make_async_copy(src, outs[i].at[slot], sems[3 * i + 2].at[0])
        copy.start()
        locals_.append(copy)

    later = []
    for i, kind in enumerate(kinds):
        src = ins[i]
        if kind == "tag":
            for k in (1, 3, 2):
                send(i, src, at.t, k, ("t", 0, k))
            for j in (1, 3, 2):
                send(i, src, at.t, 4 * j, ("t", j, 0))
            keep(i, src, at.t)

            def forward(i=i):
                for k in (1, 3, 2):
                    slot = at.tile(0, 4 - k)
                    arrive(i, slot, k, ("t", 0, k))
                    for j in (1, 3, 2):
                        send(i, outs[i].at[slot], slot, 4 * j + k, ("t", j, 0))

            def finish(i=i):
                for k in range(4):
                    for j in (1, 3, 2):
                        arrive(i, at.tile(4 - j, 4 - k), 4 * j + k, ("t", j, 0))

            later.append((forward, finish))
        elif kind == "hag":
            send(i, src, at.h, 4, ("h", 0, 2))
            for j in (1, 3, 2):
                send(i, src, at.h, j, ("h", j, 0))
            send(i, src, at.h, 8, ("h", 0, 1))
            keep(i, src, at.h)

            def forward(i=i):
                slot = at.head(0, 2)
                arrive(i, slot, 4, ("h", 0, 2))
                for j in (1, 3, 2):
                    send(i, outs[i].at[slot], slot, 4 + j, ("h", j, 0))
                send(i, outs[i].at[slot], slot, 12, ("h", 0, 1))

            def finish(i=i):
                for z in (0, 1):
                    for j in (1, 3, 2):
                        slot = at.head(4 - j, 2 * z)
                        arrive(i, slot, 4 * z + j, ("h", j, 0))
                        send(i, outs[i].at[slot], slot, 8 + 4 * z + j, ("h", 0, 1))
                for z in (0, 1):
                    for j in range(4):
                        arrive(i, at.head(4 - j, 2 * z + 1), 8 + 4 * z + j, ("h", 0, 1))

            later.append((forward, finish))
        elif kind == "ha2a":
            for f in (3, 2, 1, 0):
                for j in range(4):
                    if f or j:
                        send(i, src.at[at.head(j, f)], at.h, 4 * f + j, ("h", j, f))
            keep(i, src.at[at.h], at.h)

            def finish(i=i):
                for f in range(4):
                    for j in range(4):
                        if f or j:
                            arrive(i, at.head(4 - j, f), 4 * f + j, ("h", j, f))

            later.append((None, finish))
        else:
            along_z = kind == "za2a"

            def spot(j):
                return lax.rem((at.b if along_z else at.a) + j, SIDE)

            def piece(j):
                if kind == "yag":
                    return src
                if kind == "ycols":
                    width = src.shape[1] // SIDE
                    return src.at[:, pl.ds(pl.multiple_of(spot(j) * width, 128), width)]
                return src.at[spot(j)]

            def peer_of(j, along_z=along_z):
                return ("t", 0, j) if along_z else ("t", j, 0)

            mine = spot(0)
            for j in (1, 3, 2):
                send(i, piece(j), mine, j, peer_of(j))
            keep(i, piece(0), mine)
            froms = {j: spot(4 - j) for j in (1, 2, 3)}

            def finish(i=i, froms=froms, peer_of=peer_of):
                for j in (1, 3, 2):
                    arrive(i, froms[j], j, peer_of(j))

            later.append((None, finish))

    for forward, _ in later:
        if forward is not None:
            forward()
    for _, finish in later:
        finish()
    for copy in started:
        copy.wait_send()
    for copy in locals_:
        copy.wait()


def exchange(name, cid, *tasks):
    kinds = tuple(kind for kind, _ in tasks)
    arrays = [array for _, array in tasks]
    shapes = []
    for kind, array in tasks:
        if kind in ("tag", "hag", "yag"):
            piece = array.shape
        elif kind == "ycols":
            piece = (array.shape[0], array.shape[1] // SIDE)
        else:
            piece = array.shape[1:]
        shapes.append(jax.ShapeDtypeStruct((out_slots(kind),) + piece, array.dtype))
    scratch = []
    for kind in kinds:
        scratch += [
            pltpu.SemaphoreType.DMA((TASK_SEMS[kind],)),
            pltpu.SemaphoreType.DMA((TASK_SEMS[kind],)),
            pltpu.SemaphoreType.DMA((1,)),
        ]
    return pl.pallas_call(
        functools.partial(comm_kernel, kinds),
        out_shape=shapes,
        in_specs=[pl.BlockSpec(memory_space=pltpu.VMEM)] * len(arrays),
        out_specs=[pl.BlockSpec(memory_space=pl.ANY)] * len(arrays),
        scratch_shapes=scratch,
        compiler_params=pltpu.CompilerParams(
            collective_id=cid, has_side_effects=True, vmem_limit_bytes=16 * 1024 * 1024
        ),
        name=name,
    )(*arrays)


def near(first, second):
    def coords(ids):
        return ids // (TH * TW), ids // TW % TH, ids % TW

    close = True
    for one, two in zip(coords(first), coords(second)):
        close = close & (jnp.abs(one - two) <= 1)
    return close


def attend_kernel(slots_ref, query_ref, kv_ref, att_ref, inv_ref, exp_ref, total_ref, acc_ref):
    mine = slots_ref[lax.axis_index("tile")]
    total_ref[...] = jnp.zeros_like(total_ref)
    acc_ref[...] = jnp.zeros_like(acc_ref)
    count = kv_ref.shape[0]

    @pl.loop(0, count)
    def _(j):
        @pl.when(near(mine, slots_ref[j]))
        def _():
            scores = lax.dot_general(
                query_ref[...], kv_ref[j, :, :HD], NT, preferred_element_type=F32
            )
            grown = jnp.exp(scores * ATT_SCALE)
            exp_ref[j] = grown
            total_ref[...] += jnp.sum(grown, -1, keepdims=True)

    inv = 1.0 / total_ref[...]
    inv_ref[...] = jnp.broadcast_to(inv, inv_ref.shape)

    @pl.loop(0, count)
    def _(j):
        @pl.when(near(mine, slots_ref[j]))
        def _():
            probs = (exp_ref[j] * inv).astype(BF16)
            acc_ref[...] += jnp.dot(probs, kv_ref[j, :, HD:], preferred_element_type=F32)

    att_ref[...] = acc_ref[...].astype(BF16)


def attend(slots, query_b, all_kv):
    rows = query_b.shape[0]
    return pl.pallas_call(
        attend_kernel,
        out_shape=(
            jax.ShapeDtypeStruct((rows, HD), BF16),
            jax.ShapeDtypeStruct((rows, HD), F32),
        ),
        in_specs=[
            pl.BlockSpec(memory_space=pltpu.SMEM),
            pl.BlockSpec(memory_space=pltpu.VMEM),
            pl.BlockSpec(memory_space=pltpu.VMEM),
        ],
        out_specs=(
            pl.BlockSpec(memory_space=pltpu.VMEM),
            pl.BlockSpec(memory_space=pltpu.VMEM),
        ),
        scratch_shapes=[
            pltpu.VMEM((all_kv.shape[0], rows, rows), F32),
            pltpu.VMEM((rows, 1), F32),
            pltpu.VMEM((rows, HD), F32),
        ],
        compiler_params=pltpu.CompilerParams(vmem_limit_bytes=VMEM_LIMIT),
        name="attend",
    )(slots, query_b, all_kv)


def branch_kernel(weight_ref, att_ref, teacher_ref, gate_ref, grad_ref):
    total = None
    for h in range(att_ref.shape[0]):
        term = lax.dot_general(weight_ref[h], att_ref[h], NT, preferred_element_type=F32)
        total = term if total is None else total + term
    gate = gate_ref[...]
    residual = LOSS_WEIGHT * (gate * total - teacher_ref[...].astype(F32))
    grad_ref[...] = (gate * residual).astype(BF16)


def branch_grad(weight_parts, att_parts, teacher_part, gate_part):
    return pl.pallas_call(
        branch_kernel,
        out_shape=jax.ShapeDtypeStruct(teacher_part.shape, BF16),
        in_specs=[pl.BlockSpec(memory_space=pltpu.VMEM)] * 4,
        out_specs=pl.BlockSpec(memory_space=pltpu.VMEM),
        compiler_params=pltpu.CompilerParams(vmem_limit_bytes=VMEM_LIMIT),
        name="branch_grad",
    )(weight_parts, att_parts, teacher_part, gate_part)


def out_kernel(grad_ref, weight_ref, att_ref, inv_ref, term_ref, gatt_ref, stats_ref, delta_ref):
    rows = att_ref.shape[0]
    step = grad_ref.shape[1]
    grad_t = jnp.zeros((HD, rows), F32)
    for h in range(grad_ref.shape[0]):
        block = grad_ref[h]
        grad_t += jnp.dot(
            weight_ref[:, h * step : (h + 1) * step], block, preferred_element_type=F32
        )
        term_ref[h // SIDE, (h % SIDE) * step : (h % SIDE + 1) * step, :] = jnp.dot(
            block, att_ref[...], preferred_element_type=F32
        )
    gatt = grad_t.T.astype(BF16)
    gatt_ref[...] = gatt
    delta = jnp.sum(gatt.astype(F32) * att_ref[...].astype(F32), -1, keepdims=True)
    delta_all = jnp.broadcast_to(delta, (rows, HD))
    delta_ref[...] = delta_all
    stats_ref[0:8, :] = inv_ref[...].T[0:8]
    stats_ref[8:16, :] = delta_all.T[0:8]


def out_grads(grad_parts, out_weight, attended, inv):
    rows = attended.shape[0]
    parts, step = grad_parts.shape[:2]
    return pl.pallas_call(
        out_kernel,
        out_shape=(
            jax.ShapeDtypeStruct((SIDE, parts // SIDE * step, HD), F32),
            jax.ShapeDtypeStruct((rows, HD), BF16),
            jax.ShapeDtypeStruct((16, rows), F32),
            jax.ShapeDtypeStruct((rows, HD), F32),
        ),
        in_specs=[pl.BlockSpec(memory_space=pltpu.VMEM)] * 4,
        out_specs=(pl.BlockSpec(memory_space=pltpu.VMEM),) * 4,
        compiler_params=pltpu.CompilerParams(vmem_limit_bytes=VMEM_LIMIT),
        name="out_grads",
    )(grad_parts, out_weight, attended, inv)


def root_back(grad_unit, values):
    factor = lax.rsqrt(jnp.mean(values * values, -1, keepdims=True) + EPS_ROOT)
    unit = values * factor
    return factor * (grad_unit - unit * jnp.mean(grad_unit * unit, -1, keepdims=True))


def back_kernel(
    slots_ref,
    proj_ref,
    query_ref,
    kv_ref,
    gatt_ref,
    stats_ref,
    inv_ref,
    delta_ref,
    out_ref,
    dq_ref,
    dk_ref,
    dv_ref,
):
    me = lax.axis_index("tile")
    mine = slots_ref[me]
    dq_ref[...] = jnp.zeros_like(dq_ref)
    dk_ref[...] = jnp.zeros_like(dk_ref)
    dv_ref[...] = jnp.zeros_like(dv_ref)
    my_inv = inv_ref[:, 0:1]
    my_delta = delta_ref[:, 0:1]

    @pl.loop(0, kv_ref.shape[0])
    def _(j):
        @pl.when(near(mine, slots_ref[j]))
        def _():
            key_j = kv_ref[j, :, :HD]
            scores = lax.dot_general(query_ref[me], key_j, NT, preferred_element_type=F32)
            probs = jnp.exp(scores * ATT_SCALE) * my_inv
            gprobs = lax.dot_general(
                gatt_ref[me], kv_ref[j, :, HD:], NT, preferred_element_type=F32
            )
            gscores = (probs * (gprobs - my_delta)).astype(BF16)
            dq_ref[...] += jnp.dot(gscores, key_j, preferred_element_type=F32)

            query_j = query_ref[j]
            gatt_j = gatt_ref[j]
            scores_t = lax.dot_general(
                kv_ref[me, :, :HD], query_j, NT, preferred_element_type=F32
            )
            probs_t = jnp.exp(scores_t * ATT_SCALE) * stats_ref[j, 0:1, :]
            dv_ref[...] += jnp.dot(probs_t.astype(BF16), gatt_j, preferred_element_type=F32)
            gprobs_t = lax.dot_general(
                kv_ref[me, :, HD:], gatt_j, NT, preferred_element_type=F32
            )
            gscores_t = (probs_t * (gprobs_t - stats_ref[j, 8:9, :])).astype(BF16)
            dk_ref[...] += jnp.dot(gscores_t, query_j, preferred_element_type=F32)

    out_ref[:, :HD] = root_back(dq_ref[...] * ATT_SCALE, proj_ref[:, :HD]).astype(BF16)
    out_ref[:, HD : 2 * HD] = root_back(
        dk_ref[...] * ATT_SCALE, proj_ref[:, HD : 2 * HD]
    ).astype(BF16)
    out_ref[:, 2 * HD :] = dv_ref[...].astype(BF16)


def attend_back(slots, projected, all_query, all_kv, all_gatt, all_stats, inv, delta):
    rows = projected.shape[0]
    return pl.pallas_call(
        back_kernel,
        out_shape=jax.ShapeDtypeStruct((rows, 3 * HD), BF16),
        in_specs=[pl.BlockSpec(memory_space=pltpu.SMEM)]
        + [pl.BlockSpec(memory_space=pltpu.VMEM)] * 7,
        out_specs=pl.BlockSpec(memory_space=pltpu.VMEM),
        scratch_shapes=[pltpu.VMEM((rows, HD), F32)] * 3,
        compiler_params=pltpu.CompilerParams(vmem_limit_bytes=VMEM_LIMIT),
        name="attend_back",
    )(slots, projected, all_query, all_kv, all_gatt, all_stats, inv, delta)


def modulated_norm(tokens, mod_shift, mod_scale):
    values_in = tokens.astype(F32)
    center = values_in - jnp.mean(values_in, -1, keepdims=True)
    spread = jnp.mean(center * center, -1, keepdims=True)
    return (center * lax.rsqrt(spread + EPS_NORM) * (1.0 + mod_scale) + mod_shift).astype(BF16)


def root_norm(values):
    return values * lax.rsqrt(jnp.mean(values * values, -1, keepdims=True) + EPS_ROOT)


def per_device(tokens, mod_shift, mod_scale, mod_gate, qkv_weight, out_weight, teacher, slot_tiles):
    width = out_weight.shape[1]
    step = width // 16
    head = lax.axis_index("head")
    normed = modulated_norm(tokens, mod_shift, mod_scale)
    projected = jnp.dot(normed, qkv_weight, preferred_element_type=F32)
    query_b = root_norm(projected[:, :HD]).astype(BF16)
    key_b = root_norm(projected[:, HD : 2 * HD]).astype(BF16)
    kv = jnp.concatenate([key_b, projected[:, 2 * HD :].astype(BF16)], 1)
    weight_t = out_weight.T.reshape(16, step, HD)
    teacher_part = lax.dynamic_slice_in_dim(teacher, head * step, step, 1).T
    gate_part = lax.dynamic_slice_in_dim(mod_gate, head * step, step, 0)[:, None]

    all_kv, weight_parts = exchange("share_kv", 1, ("tag", kv), ("ha2a", weight_t))
    attended, inv = attend(slot_tiles, query_b, all_kv)
    att_parts, all_query = exchange("share_att", 2, ("hag", attended), ("tag", query_b))
    grad_part = branch_grad(weight_parts, att_parts, teacher_part, gate_part)
    grad_parts, normed_parts = exchange("share_grad", 3, ("hag", grad_part), ("ycols", normed))
    out_term, gatt, stats, delta = out_grads(grad_parts, out_weight, attended, inv)
    all_gatt, all_stats = exchange("share_gatt", 4, ("tag", gatt), ("tag", stats))
    grad_qkv = attend_back(
        slot_tiles, projected, all_query, all_kv, all_gatt, all_stats, inv, delta
    )
    qkv_parts, out_parts = exchange("share_qkv", 5, ("yag", grad_qkv), ("ya2a", out_term))
    qkv_term = lax.dot_general(
        normed_parts.reshape(-1, width // SIDE),
        qkv_parts.reshape(-1, 3 * HD),
        (((0,), (0,)), ((), ())),
        preferred_element_type=F32,
    )
    out_sum = jnp.sum(out_parts, 0).reshape(SIDE, step, HD)
    qkv_pieces, out_pieces = exchange(
        "share_sums",
        6,
        ("za2a", qkv_term.reshape(SIDE, step, 3 * HD)),
        ("za2a", out_sum),
    )
    return (jnp.sum(qkv_pieces, 0), jnp.sum(out_pieces, 0).T)


def solution(mesh):
    return jax.shard_map(
        per_device,
        mesh=mesh,
        in_specs=(
            P("tile", None),
            P(),
            P(),
            P(),
            P(None, "head"),
            P("head", None),
            P("tile", None),
            P(),
        ),
        out_specs=(P("tile", "head"), P("head", "tile")),
        check_vma=False,
    )
```

time: 682 us -> 274 us (0.40)
  waiting for transfers between devices: 603 us -> 0 us
  Pallas kernels: 0 us -> 228 us
  matrix products: 46 us -> 5.45 us
  local copies, waits for them, and re-layouts: 3.58 us -> 28.6 us
  between operations: 17.2 us -> 0.89 us
    reduce_scatter x4 -> x0, waiting for transfers between devices: 362 us -> none  [the longest x1 102 us: per_device(): lax.psum_scatter(qkv_term, 'tile', scatter_dimension=0, tiled=True)]
    pallas_call x0 -> x10, Pallas kernels: none -> 228 us  [the longest x6 202 us: exchange(): pl.pallas_call(functools.partial(comm_kernel, kinds), out_shape=shapes, i...]
    psum x1 -> x0, waiting for transfers between devices: 132 us -> none  [per_device(): whole_branch = lax.psum(partial_branch, 'head')]
    all_gather x2 -> x0, waiting for transfers between devices: 109 us -> none  [the longest x1 56.9 us: per_device(): lax.all_gather(key_b, 'tile', axis=0, tiled=True)]
    dot_general x11 -> x2, matrix products: 46 us -> 5.45 us  [the longest x1 4.05 us: per_device(): lax.dot_general(normed_parts.reshape(-1, width // SIDE), qkv_parts.reshap...]
    unnamed x24 -> x51, local copies, waits for them, and re-layouts: 2.85 us -> 20 us
  transfers between devices with their start and end apart: 7 -> 0, of which waited for: 7 -> 0; matrix products, arithmetic and copies ran while one was open for 4% -> 0% of each run, Pallas kernels for 0% -> 0%
where the time goes in v1:
time: 274 us
  Pallas kernels  228 us (83%)
  local copies, waits for them, and re-layouts  28.6 us (10%)
  other arithmetic  11.1 us (4%)
  matrix products  5.45 us (2%)
    pallas_call x6, Pallas kernels, exchange(): pl.pallas_call(functools.partial(comm_kernel, kinds), out_shape=shapes, i...  202 us
    unnamed x51, local copies, waits for them, and re-layouts  20 us
    pallas_call x1, Pallas kernels, attend_back(): pl.pallas_call(back_kernel, out_shape=jax.ShapeDtypeStruct((rows, 3 * HD)...  10.4 us
    pallas_call x1, Pallas kernels, attend(): pl.pallas_call(attend_kernel, out_shape=(jax.ShapeDtypeStruct((rows, HD),...  7.36 us

profile of v1, /device:TPU:4, one launch (start us, length us, event | category | flops | bytes accessed | tf_op | source)
XLA Modules:
  0.0 273.8 jit_solution(13626422729545356054)
XLA Ops:
  0.6 0.0 copy-start
  0.6 0.0 copy-start.21
  0.7 0.9 dynamic_slice.7
  1.6 2.2 convert_reduce_fusion
  3.8 0.0 copy-done.21
  3.8 0.0 copy-start.24
  3.8 0.8 fusion.2
  4.6 0.8 copy.22.gate_ref
  5.4 1.1 constant_dynamic-slice_fusion
  6.5 0.8 copy.26
  7.3 1.5 copy.19
  8.8 2.8 %fusion.5.refs_1_ = bf16[384,3072]{1,0:T(8,128)(2,1)S(1)} fusion(bf16[384,3072]{1,0:T(8,128)(2,1)} %param.8, f32[3072]{0:T(1024)S(1)} %copy-done.24, f32[3072]{0:T(1024)S(1)} %broadcast_add_fusion, f32[384]{0:T(512)S(1)} %add_rsqrt_fusion.2, f32[384]{0:T(512)S(1)} %broadcast_multiply_fusion), kind=kLoop, calls=%fused_computation.7 | loop fusion | flops 7077888 | bytes 4746240 | tf_op jit(solution)/shard_map/convert_element_type | solution.py:462
  11.6 1.4 fusion.6.proj_ref
  13.1 0.0 copy-done.2
  13.1 0.2 multiply_reduce_fusion
  13.3 0.8 multiply_convert_fusion
  14.1 45.5 %share_kv.1 = (bf16[16,384,256]{2,1,0:T(8,128)(2,1)S(1)}, bf16[16,192,128]{2,1,0:T(8,128)(2,1)S(1)}) custom-call(bf16[384,256]{1,0:T(8,128)(2,1)S(1)} %pad_maximum_fusion.refs_0_, bf16[16,192,128]{2,1,0:T(8,128)(2,1)S(1)} %bitcast.17), custom_call_target="tpu_custom_call" | custom-call | tf_op jit(solution)/shard_map/share_kv/pallas_call | solution.py:243
  59.7 1.6 copy-done.1
  61.3 0.9 copy-done.15
  62.2 7.4 %attend.1 = (bf16[384,128]{1,0:T(8,128)(2,1)}, f32[384,128]{1,0:T(8,128)}) custom-call(s32[16]{0:T(128)} %slots_ref.3, bf16[384,128]{1,0:T(8,128)(2,1)} %get-tuple-element.40.query_ref.refs_1_, bf16[16,384,256]{2,1,0:T(8,128)(2,1)} %copy-done.1), custom_call_target="tpu_custom_call" | custom-call | tf_op jit(solution)/shard_map/attend/pallas_call | solution.py:298
  69.5 0.9 copy-done.18
  70.4 24.7 %share_att.1 = (bf16[16,384,128]{2,1,0:T(8,128)(2,1)S(1)}, bf16[16,384,128]{2,1,0:T(8,128)(2,1)S(1)}) custom-call(bf16[384,128]{1,0:T(8,128)(2,1)S(1)} %copy-done.18, bf16[384,128]{1,0:T(8,128)(2,1)S(1)} %copy-done.14), custom_call_target="tpu_custom_call" | custom-call | tf_op jit(solution)/shard_map/share_att/pallas_call | solution.py:243
  95.2 1.2 copy-done.8
  96.4 1.1 copy-done.9
  97.5 3.2 %branch_grad.1.refs_0_ = bf16[192,384]{1,0:T(8,128)(2,1)} custom-call(bf16[16,192,128]{2,1,0:T(8,128)(2,1)} %copy-done.15, bf16[16,384,128]{2,1,0:T(8,128)(2,1)} %copy-done.8, bf16[192,384]{1,0:T(8,128)(2,1)} %bitcast.23, f32[192,1]{1,0:T(8,128)} %copy.22.gate_ref), custom_call_target="tpu_custom_call" | custom-call | tf_op jit(solution)/shard_map/branch_grad/pallas_call | solution.py:334
  100.7 1.7 copy-done.3
  102.3 0.9 copy-done.16
  103.2 29.7 %share_grad.1 = (bf16[16,192,384]{2,1,0:T(8,128)(2,1)S(1)}, bf16[4,384,768]{2,1,0:T(8,128)(2,1)S(1)}) custom-call(bf16[192,384]{1,0:T(8,128)(2,1)S(1)} %copy-done.16, bf16[384,3072]{1,0:T(8,128)(2,1)S(1)} %copy-done.3), custom_call_target="tpu_custom_call" | custom-call | tf_op jit(solution)/shard_map/share_grad/pallas_call | solution.py:243
  133.0 1.5 copy-done.4
  134.4 1.4 copy-done.5
  135.8 4.3 %copy.23 = bf16[768,1536]{1,0:T(8,128)(2,1)} copy(bf16[768,1536]{0,1:T(8,128)(2,1)} %bitcast.18) | data formatting | bytes 4718592 | tf_op jit(solution)/shard_map/dot_general | solution.py:493
  140.1 4.6 %out_grads.1 = (f32[4,768,128]{2,1,0:T(8,128)}, bf16[384,128]{1,0:T(8,128)(2,1)}, f32[16,384]{1,0:T(8,128)}, f32[384,128]{1,0:T(8,128)}) custom-call(bf16[16,192,384]{2,1,0:T(8,128)(2,1)} %copy-done.5, bf16[128,3072]{1,0:T(8,128)(2,1)} %weight_ref.1, bf16[384,128]{1,0:T(8,128)(2,1)} %get-tuple-element.22.refs_0_.att_ref, f32[384,128]{1,0:T(8,128)} %get-tuple-element.27.inv_ref), custom_call_target="tpu_custom_call" | custom-call | tf_op jit(solution)/shard_map/out_grads/pallas_call | solution.py:368
  144.7 0.9 copy-done.19
  145.6 0.7 copy-done.20
  146.4 29.5 %share_gatt.1 = (bf16[16,384,128]{2,1,0:T(8,128)(2,1)S(1)}, f32[16,16,384]{2,1,0:T(8,128)S(1)}) custom-call(bf16[384,128]{1,0:T(8,128)(2,1)S(1)} %copy-done.19, f32[16,384]{1,0:T(8,128)S(1)} %copy-done.20), custom_call_target="tpu_custom_call" | custom-call | tf_op jit(solution)/shard_map/share_gatt/pallas_call | solution.py:243
  175.8 1.2 copy-done.10
  177.0 0.7 copy-done.17
  177.8 10.4 %attend_back.1.refs_0_ = bf16[384,384]{1,0:T(8,128)(2,1)} custom-call(s32[16]{0:T(128)} %slots_ref.3, f32[384,384]{1,0:T(8,128)} %copy-done.22, bf16[16,384,128]{2,1,0:T(8,128)(2,1)} %copy-done.9, bf16[16,384,256]{2,1,0:T(8,128)(2,1)} %copy-done.1, bf16[16,384,128]{2,1,0:T(8,128)(2,1)} %copy-done.10, f32[16,16,384]{2,1,0:T(8,128)} %copy-done.17, ...), custom_call_target="tpu_custom_call" | custom-call | tf_op jit(solution)/shard_map/attend_back/pallas_call | solution.py:446
  188.2 1.0 copy-done.11
  189.2 32.8 %share_qkv.1 = (bf16[4,384,384]{2,1,0:T(8,128)(2,1)S(1)}, f32[4,768,128]{2,1,0:T(8,128)S(1)}) custom-call(bf16[384,384]{1,0:T(8,128)(2,1)S(1)} %copy-done.11, f32[4,768,128]{2,1,0:T(8,128)S(1)} %copy-done.6), custom_call_target="tpu_custom_call" | custom-call | tf_op jit(solution)/shard_map/share_qkv/pallas_call | solution.py:243
  221.9 1.2 copy-done.7
  223.1 4.1 %fusion.7.refs_0_ = f32[4,192,384]{2,1,0:T(8,128)} fusion(bf16[4,192,1536]{2,1,0:T(8,128)(2,1)} %bitcast.22, bf16[1536,384,1]{1,0,2:T(8,128)(2,1)S(1)} %bitcast.20), kind=kOutput, calls=%fused_computation.21 | convolution fusion | flops 905969664 | bytes 4718592 | tf_op jit(solution)/shard_map/dot_general | solution.py:493
  227.2 1.5 reduce_sum.67
  228.7 1.3 copy-done.12
  230.0 40.0 %share_sums.1 = (f32[4,192,384]{2,1,0:T(8,128)S(1)}, f32[4,192,128]{2,1,0:T(8,128)S(1)}) custom-call(f32[4,192,384]{2,1,0:T(8,128)S(1)} %copy-done.12, f32[4,192,128]{2,1,0:T(8,128)S(1)} %bitcast.19), custom_call_target="tpu_custom_call" | custom-call | tf_op jit(solution)/shard_map/share_sums/pallas_call | solution.py:243
  270.0 1.0 copy-done.13
  271.0 2.1 reduce_sum.68
  273.1 0.7 reduce_sum.69
  (34 shorter events, 0.1 us)
Async XLA Ops:
  0.6 11.0 %copy-start = (bf16[3072,384]{1,0:T(8,128)(2,1)S(1)}, bf16[3072,384]{1,0:T(8,128)(2,1)}, u32[]{:S(2)}) copy-start(bf16[3072,384]{1,0:T(8,128)(2,1)} %param.12) | copy-start | bytes 7077892
  0.6 3.2 %copy-start.21 = (bf16[384,3072]{1,0:T(8,128)(2,1)S(1)}, bf16[384,3072]{1,0:T(8,128)(2,1)}, u32[]{:S(2)}) copy-start(bf16[384,3072]{1,0:T(8,128)(2,1)} %param.8) | copy-start | bytes 7077892
  1.6 3.0 %copy-start.23 = (f32[3072]{0:T(1024)S(1)}, f32[3072]{0:T(1024)}, u32[]{:S(2)}) copy-start(f32[3072]{0:T(1024)} %param.10) | copy-start | bytes 36868
  3.8 5.0 %copy-start.24 = (f32[3072]{0:T(1024)S(1)}, f32[3072]{0:T(1024)}, u32[]{:S(2)}) copy-start(f32[3072]{0:T(1024)} %param.9) | copy-start | bytes 36868
  11.6 1.5 copy-start.2
  13.1 1.0 copy-start.22
  14.1 55.4 %copy-start.14 = (bf16[384,128]{1,0:T(8,128)(2,1)S(1)}, bf16[384,128]{1,0:T(8,128)(2,1)}, u32[]{:S(2)}) copy-start(bf16[384,128]{1,0:T(8,128)(2,1)} %get-tuple-element.40.query_ref.refs_1_) | copy-start | bytes 294916
  59.6 1.6 copy-start.1
  61.3 0.9 copy-start.15
  69.5 0.9 copy-start.18
  95.2 1.2 copy-start.8
  96.4 1.1 copy-start.9
  100.7 1.7 copy-start.3
  102.3 0.9 copy-start.16
  132.9 1.5 copy-start.4
  134.4 1.4 copy-start.5
  144.7 0.9 copy-start.19
  145.6 0.7 copy-start.20
  175.8 1.2 copy-start.10
  177.0 0.7 copy-start.17
  177.8 10.4 %copy-start.6 = (f32[4,768,128]{2,1,0:T(8,128)S(1)}, f32[4,768,128]{2,1,0:T(8,128)}, u32[]{:S(2)}) copy-start(f32[4,768,128]{2,1,0:T(8,128)} %get-tuple-element.33.refs_1_) | copy-start | bytes 4718596
  188.2 1.0 copy-start.11
  221.9 1.2 copy-start.7
  228.7 1.3 copy-start.12
  270.0 1.0 copy-start.13

commit v2 on v1

--- a/solution.py
+++ b/solution.py
@@ -21,7 +21,7 @@
 F32 = jnp.float32
 MESH = pl.DeviceIdType.MESH
 NT = (((1,), (1,)), ((), ()))
-VMEM_LIMIT = 60 * 1024 * 1024
+VMEM_LIMIT = 32 * 1024 * 1024
 
 
 class Places:
@@ -46,18 +46,22 @@
         return lax.rem(self.x + j, 4) * 4 + lo
 
 
-TASK_SEMS = {"tag": 16, "hag": 16, "ha2a": 16, "ycols": 4, "yag": 4, "ya2a": 4, "za2a": 4}
+TASK_SEMS = {"tag": 20, "hag": 18, "ha2a": 16, "ycols": 8, "yag": 5, "ya2a": 4, "za2a": 4}
 
 
 def task_peers(kind):
     if kind == "tag":
-        return {("t", 0, k) for k in (1, 2, 3)} | {("t", j, 0) for j in (1, 2, 3)}
+        return {("t", 0, k) for k in (1, 2, 3)} | {("t", j, 0) for j in (1, 3)}
     if kind == "hag":
-        return {("h", j, 0) for j in (1, 2, 3)} | {("h", 0, 2), ("h", 0, 1)}
+        return {("h", j, 0) for j in (1, 3)} | {("h", 0, 2), ("h", 0, 1)}
     if kind == "ha2a":
         return {("h", j, f) for j in range(4) for f in range(4)} - {("h", 0, 0)}
     if kind == "za2a":
         return {("t", 0, k) for k in (1, 2, 3)}
+    if kind == "yag":
+        return {("t", j, 0) for j in (1, 3)}
+    if kind == "ycols":
+        return {("t", j, 0) for j in (1, 2, 3)} | {("h", 0, 1)}
     return {("t", j, 0) for j in (1, 2, 3)}
 
 
@@ -77,12 +81,6 @@
             return (at.tile(j, k), at.h)
         return (at.t, at.head(j, k))
 
-    def back(peer):
-        axis, j, k = peer
-        if axis == "t":
-            return ("t", (4 - j) % 4, (4 - k) % 4)
-        return ("h", (4 - j) % 4, k)
-
     peers = sorted(set().union(*[task_peers(kind) for kind in kinds]))
     barrier = pltpu.get_barrier_semaphore()
     for peer in peers:
@@ -92,10 +90,10 @@
     started = []
     locals_ = []
 
-    def send(i, src, slot, index, peer):
+    def send(i, src, dst, index, peer):
         copy = pltpu.make_async_remote_copy(
             src_ref=src,
-            dst_ref=outs[i].at[slot],
+            dst_ref=dst,
             send_sem=sems[3 * i].at[index],
             recv_sem=sems[3 * i + 1].at[index],
             device_id=device(peer),
@@ -104,10 +102,10 @@
         copy.start()
         started.append(copy)
 
-    def arrive(i, slot, index, peer):
+    def arrive(i, dst, index, peer):
         pltpu.make_async_remote_copy(
-            src_ref=outs[i].at[slot],
-            dst_ref=outs[i].at[slot],
+            src_ref=dst,
+            dst_ref=dst,
             send_sem=sems[3 * i].at[index],
             recv_sem=sems[3 * i + 1].at[index],
             device_id=device(peer),
@@ -119,102 +117,171 @@
         copy.start()
         locals_.append(copy)
 
-    later = []
+    steps = []
     for i, kind in enumerate(kinds):
         src = ins[i]
-        if kind == "tag":
-            for k in (1, 3, 2):
-                send(i, src, at.t, k, ("t", 0, k))
-            for j in (1, 3, 2):
-                send(i, src, at.t, 4 * j, ("t", j, 0))
-            keep(i, src, at.t)
-
-            def forward(i=i):
+        out = outs[i]
+
+        def half(slot, part, out=out):
+            rows = out.shape[1] // 2
+            return out.at[slot, pl.ds(part * rows, rows)]
+
+        if kind in ("tag", "hag", "yag"):
+            unit = math.prod(src.shape) * src.dtype.itemsize / 45000.0
+            axis = "h" if kind == "hag" else "t"
+
+            def slot_of(j, k, kind=kind):
+                if kind == "hag":
+                    return at.head(j, 2 * k)
+                if kind == "tag":
+                    return at.tile(j, k)
+                return lax.rem(at.a + j, SIDE)
+
+            def spread(i, k, block, axis=axis, slot_of=slot_of, out=out):
+                slot = slot_of(0, 4 - k if axis == "t" and k else k)
+                for j in (1, 3):
+                    send(i, block, out.at[slot], 4 * j + k, (axis, j, 0))
+
+            def relay(i, k, axis=axis, slot_of=slot_of, half=half, out=out, kind=kind):
+                back = 4 - k if axis == "t" and k else k
+                for j, part in ((1, 0), (3, 1)):
+                    slot = slot_of(4 - j, back)
+                    arrive(i, out.at[slot], 4 * j + k, (axis, j, 0))
+                    send(i, half(slot, part), half(slot, part), (8 + k, k)[part], (axis, j, 0))
+                    if kind == "hag":
+                        send(i, out.at[slot], out.at[slot], (4 * j + 2 + k), ("h", 0, 1))
+
+            def far(i, k, axis=axis, slot_of=slot_of, half=half, out=out, kind=kind):
+                back = 4 - k if axis == "t" and k else k
+                slot = slot_of(2, back)
+                arrive(i, half(slot, 0), 8 + k, (axis, 1, 0))
+                arrive(i, half(slot, 1), k, (axis, 3, 0))
+                if kind == "hag":
+                    send(i, out.at[slot], out.at[slot], 10 + k, ("h", 0, 1))
+
+            if kind == "tag":
                 for k in (1, 3, 2):
-                    slot = at.tile(0, 4 - k)
-                    arrive(i, slot, k, ("t", 0, k))
-                    for j in (1, 3, 2):
-                        send(i, outs[i].at[slot], slot, 4 * j + k, ("t", j, 0))
-
-            def finish(i=i):
-                for k in range(4):
-                    for j in (1, 3, 2):
-                        arrive(i, at.tile(4 - j, 4 - k), 4 * j + k, ("t", j, 0))
-
-            later.append((forward, finish))
-        elif kind == "hag":
-            send(i, src, at.h, 4, ("h", 0, 2))
-            for j in (1, 3, 2):
-                send(i, src, at.h, j, ("h", j, 0))
-            send(i, src, at.h, 8, ("h", 0, 1))
-            keep(i, src, at.h)
-
-            def forward(i=i):
-                slot = at.head(0, 2)
-                arrive(i, slot, 4, ("h", 0, 2))
-                for j in (1, 3, 2):
-                    send(i, outs[i].at[slot], slot, 4 + j, ("h", j, 0))
-                send(i, outs[i].at[slot], slot, 12, ("h", 0, 1))
-
-            def finish(i=i):
-                for z in (0, 1):
-                    for j in (1, 3, 2):
-                        slot = at.head(4 - j, 2 * z)
-                        arrive(i, slot, 4 * z + j, ("h", j, 0))
-                        send(i, outs[i].at[slot], slot, 8 + 4 * z + j, ("h", 0, 1))
-                for z in (0, 1):
-                    for j in range(4):
-                        arrive(i, at.head(4 - j, 2 * z + 1), 8 + 4 * z + j, ("h", 0, 1))
-
-            later.append((forward, finish))
+                    send(i, src, out.at[at.t], 15 + k + (k == 1) * 3, ("t", 0, k))
+                spread(i, 0, src)
+                keep(i, src, at.t)
+
+                def onward(i=i, out=out, spread=spread, ks=()):
+                    for k in ks:
+                        slot = at.tile(0, 4 - k)
+                        arrive(i, out.at[slot], 15 + k + (k == 1) * 3, ("t", 0, k))
+                        spread(i, k, out.at[slot])
+
+                steps.append((unit + 1, functools.partial(relay, i, 0)))
+                steps.append((2 * unit + 1, functools.partial(onward, ks=(1, 3))))
+                steps.append((3 * unit + 1, functools.partial(relay, i, 1)))
+                steps.append((4 * unit + 1, functools.partial(relay, i, 3)))
+                steps.append((4.5 * unit + 1, functools.partial(onward, ks=(2,))))
+                steps.append((6 * unit + 1, functools.partial(relay, i, 2)))
+                for k in (0, 1, 3, 2):
+                    steps.append((1000, functools.partial(far, i, k)))
+            elif kind == "hag":
+                send(i, src, out.at[at.h], 16, ("h", 0, 2))
+                spread(i, 0, src)
+                send(i, src, out.at[at.h], 2, ("h", 0, 1))
+                keep(i, src, at.h)
+
+                def onward(i=i, out=out, spread=spread):
+                    slot = at.head(0, 2)
+                    arrive(i, out.at[slot], 16, ("h", 0, 2))
+                    spread(i, 1, out.at[slot])
+                    send(i, out.at[slot], out.at[slot], 3, ("h", 0, 1))
+
+                def finish(i=i, out=out):
+                    for k in (0, 1):
+                        for j in range(4):
+                            slot = at.head(4 - j, 2 * k + 1)
+                            arrive(i, out.at[slot], 4 * j + 2 + k, ("h", 0, 1))
+
+                steps.append((unit, onward))
+                steps.append((unit + 1, functools.partial(relay, i, 0)))
+                steps.append((2 * unit + 1, functools.partial(relay, i, 1)))
+                for k in (0, 1):
+                    steps.append(((2.5 + k) * unit + 1, functools.partial(far, i, k)))
+                steps.append((1001, finish))
+            else:
+                for j in (1, 3):
+                    send(i, src, out.at[at.a], j, ("t", j, 0))
+                keep(i, src, at.a)
+
+                def pass_on(i=i, half=half, out=out):
+                    for j, part in ((1, 0), (3, 1)):
+                        slot = lax.rem(at.a + 4 - j, SIDE)
+                        arrive(i, out.at[slot], j, ("t", j, 0))
+                        send(i, half(slot, part), half(slot, part), (2, 4)[part], ("t", j, 0))
+
+                def finish(i=i, half=half):
+                    slot = lax.rem(at.a + 2, SIDE)
+                    arrive(i, half(slot, 0), 2, ("t", 1, 0))
+                    arrive(i, half(slot, 1), 4, ("t", 3, 0))
+
+                steps.append((unit + 1, pass_on))
+                steps.append((1000, finish))
         elif kind == "ha2a":
             for f in (3, 2, 1, 0):
                 for j in range(4):
                     if f or j:
-                        send(i, src.at[at.head(j, f)], at.h, 4 * f + j, ("h", j, f))
+                        send(i, src.at[at.head(j, f)], out.at[at.h], 4 * f + j, ("h", j, f))
             keep(i, src.at[at.h], at.h)
 
-            def finish(i=i):
+            def finish(i=i, out=out):
                 for f in range(4):
                     for j in range(4):
                         if f or j:
-                            arrive(i, at.head(4 - j, f), 4 * f + j, ("h", j, f))
-
-            later.append((None, finish))
+                            arrive(i, out.at[at.head(4 - j, f)], 4 * f + j, ("h", j, f))
+
+            steps.append((1000, finish))
+        elif kind == "ycols":
+            width = src.shape[1] // SIDE
+            rows = src.shape[0] // 2
+            mine = pl.ds(pl.multiple_of(lax.rem(at.h, 2) * rows, rows), rows)
+            other = pl.ds(pl.multiple_of((1 - lax.rem(at.h, 2)) * rows, rows), rows)
+
+            def columns(j, width=width):
+                return pl.ds(pl.multiple_of(lax.rem(at.a + j, SIDE) * width, 128), width)
+
+            for j in (2, 1, 3):
+                send(i, src.at[mine, columns(j)], out.at[at.a, mine], j, ("t", j, 0))
+            keep(i, src.at[:, columns(0)], at.a)
+
+            def share(i=i, out=out, mine=mine):
+                for j in (1, 3, 2):
+                    block = out.at[lax.rem(at.a + 4 - j, SIDE), mine]
+                    arrive(i, block, j, ("t", j, 0))
+                    send(i, block, block, 4 + j, ("h", 0, 1))
+
+            def finish(i=i, out=out, other=other):
+                for j in (1, 3, 2):
+                    block = out.at[lax.rem(at.a + 4 - j, SIDE), other]
+                    arrive(i, block, 4 + j, ("h", 0, 1))
+
+            steps.append((999, share))
+            steps.append((1002, finish))
         else:
             along_z = kind == "za2a"
 
-            def spot(j):
+            def spot(j, along_z=along_z):
                 return lax.rem((at.b if along_z else at.a) + j, SIDE)
-
-            def piece(j):
-                if kind == "yag":
-                    return src
-                if kind == "ycols":
-                    width = src.shape[1] // SIDE
-                    return src.at[:, pl.ds(pl.multiple_of(spot(j) * width, 128), width)]
-                return src.at[spot(j)]
 
             def peer_of(j, along_z=along_z):
                 return ("t", 0, j) if along_z else ("t", j, 0)
 
-            mine = spot(0)
             for j in (1, 3, 2):
-                send(i, piece(j), mine, j, peer_of(j))
-            keep(i, piece(0), mine)
-            froms = {j: spot(4 - j) for j in (1, 2, 3)}
-
-            def finish(i=i, froms=froms, peer_of=peer_of):
+                send(i, src.at[spot(j)], out.at[spot(0)], j, peer_of(j))
+            keep(i, src.at[spot(0)], spot(0))
+
+            def finish(i=i, out=out, spot=spot, peer_of=peer_of):
                 for j in (1, 3, 2):
-                    arrive(i, froms[j], j, peer_of(j))
-
-            later.append((None, finish))
-
-    for forward, _ in later:
-        if forward is not None:
-            forward()
-    for _, finish in later:
-        finish()
+                    arrive(i, out.at[spot(4 - j)], j, peer_of(j))
+
+            steps.append((1000, finish))
+
+    for _, step in sorted(steps, key=lambda step: step[0]):
+        step()
     for copy in started:
         copy.wait_send()
     for copy in locals_:
@@ -244,7 +311,7 @@
         functools.partial(comm_kernel, kinds),
         out_shape=shapes,
         in_specs=[pl.BlockSpec(memory_space=pltpu.VMEM)] * len(arrays),
-        out_specs=[pl.BlockSpec(memory_space=pl.ANY)] * len(arrays),
+        out_specs=[pl.BlockSpec(memory_space=pltpu.VMEM)] * len(arrays),
         scratch_shapes=scratch,
         compiler_params=pltpu.CompilerParams(
             collective_id=cid, has_side_effects=True, vmem_limit_bytes=16 * 1024 * 1024

time: 274 us -> 248 us (0.905)
  the two profiles are of different devices: /device:TPU:4 before, /device:TPU:2 now
where the time goes in v2:
time: 248 us
  Pallas kernels  210 us (85%)
  local copies, waits for them, and re-layouts  22.8 us (9%)
  other arithmetic  10.5 us (4%)
  matrix products  3.79 us (2%)
    pallas_call x6, Pallas kernels, exchange(): pl.pallas_call(functools.partial(comm_kernel, kinds), out_shape=shapes, i...  198 us
    unnamed x39, local copies, waits for them, and re-layouts  14.5 us
    pallas_call x1, Pallas kernels, attend_back(): pl.pallas_call(back_kernel, out_shape=jax.ShapeDtypeStruct((rows, 3 * HD)...  5.18 us

profile of v2, /device:TPU:2, one launch (start us, length us, event | category | flops | bytes accessed | tf_op | source)
XLA Modules:
  0.0 247.7 jit_solution(2645343525749132795)
XLA Ops:
  0.6 0.0 copy-start
  0.6 0.0 copy-start.15
  0.7 0.9 dynamic_slice.7
  1.6 2.2 convert_reduce_fusion
  3.8 0.0 copy-done.15
  3.8 0.0 copy-start.18
  3.8 0.8 fusion.2
  4.6 0.0 copy-done.17
  4.6 0.1 copy.22.gate_ref
  4.7 1.8 constant_dynamic-slice_fusion
  6.5 1.1 copy.26
  7.6 0.0 copy-done.3
  7.6 1.2 copy.19
  8.8 0.0 copy-done.18
  8.8 2.8 %fusion.5.refs_1_ = bf16[384,3072]{1,0:T(8,128)(2,1)S(1)} fusion(bf16[384,3072]{1,0:T(8,128)(2,1)} %param.8, f32[3072]{0:T(1024)S(1)} %copy-done.18, f32[3072]{0:T(1024)S(1)} %broadcast_add_fusion, f32[384]{0:T(512)S(1)} %add_rsqrt_fusion.2, f32[384]{0:T(512)S(1)} %broadcast_multiply_fusion), kind=kLoop, calls=%fused_computation.7 | loop fusion | flops 7077888 | bytes 4746240 | tf_op jit(solution)/shard_map/convert_element_type | solution.py:529
  11.6 0.0 copy-done
  11.6 0.0 copy-start.5
  11.6 1.4 fusion.6.proj_ref
  13.0 0.0 copy-start.14
  13.0 0.2 multiply_reduce_fusion
  13.2 0.2 multiply_convert_fusion
  13.4 0.0 copy-done.5
  13.5 42.4 %share_kv.1 = (bf16[16,384,256]{2,1,0:T(8,128)(2,1)S(1)}, bf16[16,192,128]{2,1,0:T(8,128)(2,1)S(1)}) custom-call(bf16[384,256]{1,0:T(8,128)(2,1)S(1)} %pad_maximum_fusion.refs_0_, bf16[16,192,128]{2,1,0:T(8,128)(2,1)S(1)} %bitcast.18), custom_call_target="tpu_custom_call" | custom-call | tf_op jit(solution)/shard_map/share_kv/pallas_call | solution.py:310
  55.9 4.0 %attend.1 = (bf16[384,128]{1,0:T(8,128)(2,1)S(1)}, f32[384,128]{1,0:T(8,128)S(1)}) custom-call(s32[16]{0:T(128)S(1)} %copy-done.14, bf16[384,128]{1,0:T(8,128)(2,1)S(1)} %get-tuple-element.40.query_ref.refs_1_, bf16[16,384,256]{2,1,0:T(8,128)(2,1)S(1)} %get-tuple-element.21.kv_ref), custom_call_target="tpu_custom_call" | custom-call | tf_op jit(solution)/shard_map/attend/pallas_call | solution.py:365
  60.0 1.6 copy-done.1
  61.6 30.2 %share_att.1 = (bf16[16,384,128]{2,1,0:T(8,128)(2,1)S(1)}, bf16[16,384,128]{2,1,0:T(8,128)(2,1)S(1)}) custom-call(bf16[384,128]{1,0:T(8,128)(2,1)S(1)} %get-tuple-element.22.refs_0_.att_ref, bf16[384,128]{1,0:T(8,128)(2,1)S(1)} %get-tuple-element.40.query_ref.refs_1_), custom_call_target="tpu_custom_call" | custom-call | tf_op jit(solution)/shard_map/share_att/pallas_call | solution.py:310
  91.8 1.2 copy-done.10
  93.0 0.9 branch_grad.1.refs_0_
  93.8 19.5 %share_grad.1 = (bf16[16,192,384]{2,1,0:T(8,128)(2,1)S(1)}, bf16[4,384,768]{2,1,0:T(8,128)(2,1)S(1)}) custom-call(bf16[192,384]{1,0:T(8,128)(2,1)S(1)} %branch_grad.1.refs_0_, bf16[384,3072]{1,0:T(8,128)(2,1)S(1)} %fusion.5.refs_1_), custom_call_target="tpu_custom_call" | custom-call | tf_op jit(solution)/shard_map/share_grad/pallas_call | solution.py:310
  113.4 1.4 copy-done.6
  114.8 1.5 copy-done.7
  116.2 4.3 %copy.23 = bf16[768,1536]{1,0:T(8,128)(2,1)} copy(bf16[768,1536]{0,1:T(8,128)(2,1)} %bitcast.19) | data formatting | bytes 4718592 | tf_op jit(solution)/shard_map/dot_general | solution.py:560
  120.6 1.3 copy-done.4
  121.8 1.7 copy-done.8
  123.5 1.5 out_grads.1
  125.0 39.0 %share_gatt.1 = (bf16[16,384,128]{2,1,0:T(8,128)(2,1)S(1)}, f32[16,16,384]{2,1,0:T(8,128)S(1)}) custom-call(bf16[384,128]{1,0:T(8,128)(2,1)S(1)} %get-tuple-element.28.refs_0_, f32[16,384]{1,0:T(8,128)S(1)} %get-tuple-element.29.refs_1_), custom_call_target="tpu_custom_call" | custom-call | tf_op jit(solution)/shard_map/share_gatt/pallas_call | solution.py:310
  164.0 1.4 copy-done.11
  165.4 5.2 %attend_back.1.refs_0_ = bf16[384,384]{1,0:T(8,128)(2,1)S(1)} custom-call(s32[16]{0:T(128)S(1)} %copy-done.14, f32[384,384]{1,0:T(8,128)S(1)} %fusion.6.proj_ref, bf16[16,384,128]{2,1,0:T(8,128)(2,1)S(1)} %copy-done.11, bf16[16,384,256]{2,1,0:T(8,128)(2,1)S(1)} %copy-done.2, bf16[16,384,128]{2,1,0:T(8,128)(2,1)S(1)} %get-tuple-element.30.gatt_ref, ...), custom_call_target="tpu_custom_call" | custom-call | tf_op jit(solution)/shard_map/attend_back/pallas_call | solution.py:513
  170.6 30.9 %share_qkv.1 = (bf16[4,384,384]{2,1,0:T(8,128)(2,1)S(1)}, f32[4,768,128]{2,1,0:T(8,128)S(1)}) custom-call(bf16[384,384]{1,0:T(8,128)(2,1)S(1)} %attend_back.1.refs_0_, f32[4,768,128]{2,1,0:T(8,128)S(1)} %get-tuple-element.33.refs_1_), custom_call_target="tpu_custom_call" | custom-call | tf_op jit(solution)/shard_map/share_qkv/pallas_call | solution.py:310
  201.5 1.1 copy-done.9
  202.7 2.4 fusion.7.refs_0_
  205.1 1.5 reduce_sum.67
  206.7 1.3 copy-done.12
  207.9 36.0 %share_sums.1 = (f32[4,192,384]{2,1,0:T(8,128)S(1)}, f32[4,192,128]{2,1,0:T(8,128)S(1)}) custom-call(f32[4,192,384]{2,1,0:T(8,128)S(1)} %copy-done.12, f32[4,192,128]{2,1,0:T(8,128)S(1)} %bitcast.20), custom_call_target="tpu_custom_call" | custom-call | tf_op jit(solution)/shard_map/share_sums/pallas_call | solution.py:310
  244.0 0.0 copy-start.13
  244.0 1.0 copy-done.13
  245.0 2.1 reduce_sum.68
  247.1 0.7 reduce_sum.69
  (22 shorter events, 0.1 us)
Async XLA Ops:
  0.6 11.0 %copy-start = (bf16[3072,384]{1,0:T(8,128)(2,1)S(1)}, bf16[3072,384]{1,0:T(8,128)(2,1)}, u32[]{:S(2)}) copy-start(bf16[3072,384]{1,0:T(8,128)(2,1)} %param.12) | copy-start | bytes 7077892
  0.6 3.2 %copy-start.15 = (bf16[384,3072]{1,0:T(8,128)(2,1)S(1)}, bf16[384,3072]{1,0:T(8,128)(2,1)}, u32[]{:S(2)}) copy-start(bf16[384,3072]{1,0:T(8,128)(2,1)} %param.8) | copy-start | bytes 7077892
  1.6 3.0 %copy-start.17 = (f32[3072]{0:T(1024)S(1)}, f32[3072]{0:T(1024)}, u32[]{:S(2)}) copy-start(f32[3072]{0:T(1024)} %param.10) | copy-start | bytes 36868
  1.6 6.0 %copy-start.3 = (bf16[128,3072]{1,0:T(8,128)(2,1)S(1)}, bf16[128,3072]{1,0:T(8,128)(2,1)}, u32[]{:S(2)}) copy-start(bf16[128,3072]{1,0:T(8,128)(2,1)} %weight_ref.1) | copy-start | bytes 2359300
  3.8 4.9 %copy-start.18 = (f32[3072]{0:T(1024)S(1)}, f32[3072]{0:T(1024)}, u32[]{:S(2)}) copy-start(f32[3072]{0:T(1024)} %param.9) | copy-start | bytes 36868
  11.6 1.8 copy-start.5
  13.0 42.9 %copy-start.14 = (s32[16]{0:T(128)S(1)}, s32[16]{0:T(128)}, u32[]{:S(2)}) copy-start(s32[16]{0:T(128)} %slots_ref.3) | copy-start | bytes 196
  60.0 1.6 copy-start.1
  91.8 1.2 copy-start.10
  113.4 1.4 copy-start.6
  114.8 1.5 copy-start.7
  120.6 43.5 %copy-start.2 = (bf16[16,384,256]{2,1,0:T(8,128)(2,1)S(1)}, bf16[16,384,256]{2,1,0:T(8,128)(2,1)}, u32[]{:S(2)}) copy-start(bf16[16,384,256]{2,1,0:T(8,128)(2,1)} %copy-done.1) | copy-start | bytes 9437188
  120.6 1.3 copy-start.4
  121.8 1.7 copy-start.8
  164.0 1.4 copy-start.11
  165.4 37.2 %copy-start.16 = (bf16[768,1536]{1,0:T(8,128)(2,1)S(1)}, bf16[768,1536]{1,0:T(8,128)(2,1)}, u32[]{:S(2)}) copy-start(bf16[768,1536]{1,0:T(8,128)(2,1)} %copy.23) | copy-start | bytes 7077892
  201.5 1.1 copy-start.9
  206.6 1.3 copy-start.12
  244.0 1.0 copy-start.13

commit v3 on v2

--- a/solution.py
+++ b/solution.py
@@ -21,7 +21,8 @@
 F32 = jnp.float32
 MESH = pl.DeviceIdType.MESH
 NT = (((1,), (1,)), ((), ()))
-VMEM_LIMIT = 32 * 1024 * 1024
+VMEM_LIMIT = 24 * 1024 * 1024
+COMM_LIMIT = 8 * 1024 * 1024
 
 
 class Places:
@@ -51,7 +52,7 @@
 
 def task_peers(kind):
     if kind == "tag":
-        return {("t", 0, k) for k in (1, 2, 3)} | {("t", j, 0) for j in (1, 3)}
+        return {("t", 0, 1), ("t", 0, 3), ("t", 1, 0), ("t", 3, 0)}
     if kind == "hag":
         return {("h", j, 0) for j in (1, 3)} | {("h", 0, 2), ("h", 0, 1)}
     if kind == "ha2a":
@@ -124,10 +125,11 @@
 
         def half(slot, part, out=out):
             rows = out.shape[1] // 2
+            if rows < 8:
+                return out.at[slot, :, pl.ds(*((0, 256), (256, out.shape[2] - 256))[part])]
             return out.at[slot, pl.ds(part * rows, rows)]
 
         if kind in ("tag", "hag", "yag"):
-            unit = math.prod(src.shape) * src.dtype.itemsize / 45000.0
             axis = "h" if kind == "hag" else "t"
 
             def slot_of(j, k, kind=kind):
@@ -160,23 +162,31 @@
                     send(i, out.at[slot], out.at[slot], 10 + k, ("h", 0, 1))
 
             if kind == "tag":
-                for k in (1, 3, 2):
-                    send(i, src, out.at[at.t], 15 + k + (k == 1) * 3, ("t", 0, k))
+                for k in (1, 3):
+                    send(i, src, out.at[at.t], 16 + k, ("t", 0, k))
                 spread(i, 0, src)
                 keep(i, src, at.t)
 
-                def onward(i=i, out=out, spread=spread, ks=()):
-                    for k in ks:
+                def onward(i=i, out=out, spread=spread, half=half):
+                    for k, part in ((1, 0), (3, 1)):
                         slot = at.tile(0, 4 - k)
-                        arrive(i, out.at[slot], 15 + k + (k == 1) * 3, ("t", 0, k))
+                        arrive(i, out.at[slot], 16 + k, ("t", 0, k))
+                        piece = half(slot, part)
+                        send(i, piece, piece, (16, 18)[part], ("t", 0, k))
                         spread(i, k, out.at[slot])
 
-                steps.append((unit + 1, functools.partial(relay, i, 0)))
-                steps.append((2 * unit + 1, functools.partial(onward, ks=(1, 3))))
-                steps.append((3 * unit + 1, functools.partial(relay, i, 1)))
-                steps.append((4 * unit + 1, functools.partial(relay, i, 3)))
-                steps.append((4.5 * unit + 1, functools.partial(onward, ks=(2,))))
-                steps.append((6 * unit + 1, functools.partial(relay, i, 2)))
+                def last(i=i, out=out, spread=spread, half=half):
+                    slot = at.tile(0, 2)
+                    arrive(i, half(slot, 0), 16, ("t", 0, 1))
+                    arrive(i, half(slot, 1), 18, ("t", 0, 3))
+                    spread(i, 2, out.at[slot])
+
+                steps.append((2, functools.partial(relay, i, 0)))
+                steps.append((3, onward))
+                steps.append((4.5, functools.partial(relay, i, 1)))
+                steps.append((5, last))
+                steps.append((5.5, functools.partial(relay, i, 3)))
+                steps.append((7, functools.partial(relay, i, 2)))
                 for k in (0, 1, 3, 2):
                     steps.append((1000, functools.partial(far, i, k)))
             elif kind == "hag":
@@ -197,11 +207,11 @@
                             slot = at.head(4 - j, 2 * k + 1)
                             arrive(i, out.at[slot], 4 * j + 2 + k, ("h", 0, 1))
 
-                steps.append((unit, onward))
-                steps.append((unit + 1, functools.partial(relay, i, 0)))
-                steps.append((2 * unit + 1, functools.partial(relay, i, 1)))
-                for k in (0, 1):
-                    steps.append(((2.5 + k) * unit + 1, functools.partial(far, i, k)))
+                steps.append((1, onward))
+                steps.append((1.5, functools.partial(relay, i, 0)))
+                steps.append((3.2, functools.partial(relay, i, 1)))
+                steps.append((4, functools.partial(far, i, 0)))
+                steps.append((5.2, functools.partial(far, i, 1)))
                 steps.append((1001, finish))
             else:
                 for j in (1, 3):
@@ -219,14 +229,18 @@
                     arrive(i, half(slot, 0), 2, ("t", 1, 0))
                     arrive(i, half(slot, 1), 4, ("t", 3, 0))
 
-                steps.append((unit + 1, pass_on))
+                steps.append((1, pass_on))
                 steps.append((1000, finish))
         elif kind == "ha2a":
-            for f in (3, 2, 1, 0):
-                for j in range(4):
-                    if f or j:
-                        send(i, src.at[at.head(j, f)], out.at[at.h], 4 * f + j, ("h", j, f))
+            def give(i=i, src=src, out=out, flips=()):
+                for f in flips:
+                    for j in range(4):
+                        if f or j:
+                            send(i, src.at[at.head(j, f)], out.at[at.h], 4 * f + j, ("h", j, f))
+
+            give(flips=(1, 0))
             keep(i, src.at[at.h], at.h)
+            steps.append((5, functools.partial(give, flips=(3, 2))))
 
             def finish(i=i, out=out):
                 for f in range(4):
@@ -314,7 +328,7 @@
         out_specs=[pl.BlockSpec(memory_space=pltpu.VMEM)] * len(arrays),
         scratch_shapes=scratch,
         compiler_params=pltpu.CompilerParams(
-            collective_id=cid, has_side_effects=True, vmem_limit_bytes=16 * 1024 * 1024
+            collective_id=cid, has_side_effects=True, vmem_limit_bytes=COMM_LIMIT
         ),
         name=name,
     )(*arrays)
@@ -408,25 +422,38 @@
     )(weight_parts, att_parts, teacher_part, gate_part)
 
 
-def out_kernel(grad_ref, weight_ref, att_ref, inv_ref, term_ref, gatt_ref, stats_ref, delta_ref):
+def out_kernel(
+    grad_ref,
+    weight_ref,
+    att_ref,
+    inv_ref,
+    yterm_ref,
+    zterm_ref,
+    gatt_ref,
+    stats_ref,
+    delta_ref,
+):
     rows = att_ref.shape[0]
     step = grad_ref.shape[1]
+    half = step // 2
     grad_t = jnp.zeros((HD, rows), F32)
     for h in range(grad_ref.shape[0]):
         block = grad_ref[h]
         grad_t += jnp.dot(
             weight_ref[:, h * step : (h + 1) * step], block, preferred_element_type=F32
         )
-        term_ref[h // SIDE, (h % SIDE) * step : (h % SIDE + 1) * step, :] = jnp.dot(
-            block, att_ref[...], preferred_element_type=F32
-        )
+        term = jnp.dot(block, att_ref[...], preferred_element_type=F32)
+        low = h % SIDE * half
+        yterm_ref[h // SIDE, low : low + half, :] = term[:half]
+        low = h // SIDE * half
+        zterm_ref[h % SIDE, low : low + half, :] = term[half:]
     gatt = grad_t.T.astype(BF16)
     gatt_ref[...] = gatt
     delta = jnp.sum(gatt.astype(F32) * att_ref[...].astype(F32), -1, keepdims=True)
     delta_all = jnp.broadcast_to(delta, (rows, HD))
     delta_ref[...] = delta_all
-    stats_ref[0:8, :] = inv_ref[...].T[0:8]
-    stats_ref[8:16, :] = delta_all.T[0:8]
+    stats_ref[0:4, :] = inv_ref[...].T[0:4]
+    stats_ref[4:8, :] = delta_all.T[0:4]
 
 
 def out_grads(grad_parts, out_weight, attended, inv):
@@ -435,13 +462,14 @@
     return pl.pallas_call(
         out_kernel,
         out_shape=(
-            jax.ShapeDtypeStruct((SIDE, parts // SIDE * step, HD), F32),
+            jax.ShapeDtypeStruct((SIDE, parts // SIDE * step // 2, HD), F32),
+            jax.ShapeDtypeStruct((SIDE, parts // SIDE * step // 2, HD), F32),
             jax.ShapeDtypeStruct((rows, HD), BF16),
-            jax.ShapeDtypeStruct((16, rows), F32),
+            jax.ShapeDtypeStruct((8, rows), F32),
             jax.ShapeDtypeStruct((rows, HD), F32),
         ),
         in_specs=[pl.BlockSpec(memory_space=pltpu.VMEM)] * 4,
-        out_specs=(pl.BlockSpec(memory_space=pltpu.VMEM),) * 4,
+        out_specs=(pl.BlockSpec(memory_space=pltpu.VMEM),) * 5,
         compiler_params=pltpu.CompilerParams(vmem_limit_bytes=VMEM_LIMIT),
         name="out_grads",
     )(grad_parts, out_weight, attended, inv)
@@ -498,7 +526,7 @@
             gprobs_t = lax.dot_general(
                 kv_ref[me, :, HD:], gatt_j, NT, preferred_element_type=F32
             )
-            gscores_t = (probs_t * (gprobs_t - stats_ref[j, 8:9, :])).astype(BF16)
+            gscores_t = (probs_t * (gprobs_t - stats_ref[j, 4:5, :])).astype(BF16)
             dk_ref[...] += jnp.dot(gscores_t, query_j, preferred_element_type=F32)
 
     out_ref[:, :HD] = root_back(dq_ref[...] * ATT_SCALE, proj_ref[:, :HD]).astype(BF16)
@@ -522,6 +550,69 @@
     )(slots, projected, all_query, all_kv, all_gatt, all_stats, inv, delta)
 
 
+def terms_kernel(normed_ref, grad_ref, yparts_ref, zparts_ref, qkv_ref, ysum_ref, zsum_ref):
+    step = qkv_ref.shape[1]
+    for k in range(qkv_ref.shape[0]):
+        total = None
+        for j in range(normed_ref.shape[0]):
+            term = lax.dot_general(
+                normed_ref[j, :, k * step : (k + 1) * step],
+                grad_ref[j],
+                (((0,), (0,)), ((), ())),
+                preferred_element_type=F32,
+            )
+            total = term if total is None else total + term
+        qkv_ref[k] = total
+    for parts_ref, sum_ref in ((yparts_ref, ysum_ref), (zparts_ref, zsum_ref)):
+        half = sum_ref.shape[1]
+        for k in range(sum_ref.shape[0]):
+            rows = slice(k * half, (k + 1) * half)
+            sum_ref[k] = (parts_ref[0, rows] + parts_ref[1, rows]) + (
+                parts_ref[2, rows] + parts_ref[3, rows]
+            )
+
+
+def grad_terms(normed_parts, qkv_parts, yparts, zparts):
+    step = normed_parts.shape[2] // SIDE
+    half = yparts.shape[1] // SIDE
+    return pl.pallas_call(
+        terms_kernel,
+        out_shape=(
+            jax.ShapeDtypeStruct((SIDE, step, 3 * HD), F32),
+            jax.ShapeDtypeStruct((SIDE, half, HD), F32),
+            jax.ShapeDtypeStruct((SIDE, half, HD), F32),
+        ),
+        in_specs=[pl.BlockSpec(memory_space=pltpu.VMEM)] * 4,
+        out_specs=(pl.BlockSpec(memory_space=pltpu.VMEM),) * 3,
+        compiler_params=pltpu.CompilerParams(vmem_limit_bytes=VMEM_LIMIT),
+        name="grad_terms",
+    )(normed_parts, qkv_parts, yparts, zparts)
+
+
+def sums_kernel(qkv_ref, first_ref, second_ref, qkv_out_ref, out_out_ref):
+    qkv_out_ref[...] = (qkv_ref[0] + qkv_ref[1]) + (qkv_ref[2] + qkv_ref[3])
+    first = (first_ref[0] + first_ref[1]) + (first_ref[2] + first_ref[3])
+    second = (second_ref[0] + second_ref[1]) + (second_ref[2] + second_ref[3])
+    half = first.shape[0]
+    out_out_ref[:half, :] = first
+    out_out_ref[half:, :] = second
+
+
+def final_sums(qkv_pieces, first, second):
+    step = qkv_pieces.shape[1]
+    return pl.pallas_call(
+        sums_kernel,
+        out_shape=(
+            jax.ShapeDtypeStruct((step, 3 * HD), F32),
+            jax.ShapeDtypeStruct((step, HD), F32),
+        ),
+        in_specs=[pl.BlockSpec(memory_space=pltpu.VMEM)] * 3,
+        out_specs=(pl.BlockSpec(memory_space=pltpu.VMEM),) * 2,
+        compiler_params=pltpu.CompilerParams(vmem_limit_bytes=VMEM_LIMIT),
+        name="final_sums",
+    )(qkv_pieces, first, second)
+
+
 def modulated_norm(tokens, mod_shift, mod_scale):
     values_in = tokens.astype(F32)
     center = values_in - jnp.mean(values_in, -1, keepdims=True)
@@ -551,26 +642,19 @@
     att_parts, all_query = exchange("share_att", 2, ("hag", attended), ("tag", query_b))
     grad_part = branch_grad(weight_parts, att_parts, teacher_part, gate_part)
     grad_parts, normed_parts = exchange("share_grad", 3, ("hag", grad_part), ("ycols", normed))
-    out_term, gatt, stats, delta = out_grads(grad_parts, out_weight, attended, inv)
+    yterm, zterm, gatt, stats, delta = out_grads(grad_parts, out_weight, attended, inv)
     all_gatt, all_stats = exchange("share_gatt", 4, ("tag", gatt), ("tag", stats))
     grad_qkv = attend_back(
         slot_tiles, projected, all_query, all_kv, all_gatt, all_stats, inv, delta
     )
-    qkv_parts, out_parts = exchange("share_qkv", 5, ("yag", grad_qkv), ("ya2a", out_term))
-    qkv_term = lax.dot_general(
-        normed_parts.reshape(-1, width // SIDE),
-        qkv_parts.reshape(-1, 3 * HD),
-        (((0,), (0,)), ((), ())),
-        preferred_element_type=F32,
+    qkv_parts, yparts, zparts = exchange(
+        "share_qkv", 5, ("yag", grad_qkv), ("ya2a", yterm), ("za2a", zterm)
     )
-    out_sum = jnp.sum(out_parts, 0).reshape(SIDE, step, HD)
-    qkv_pieces, out_pieces = exchange(
-        "share_sums",
-        6,
-        ("za2a", qkv_term.reshape(SIDE, step, 3 * HD)),
-        ("za2a", out_sum),
+    qkv_term, ysum, zsum = grad_terms(normed_parts, qkv_parts, yparts, zparts)
+    qkv_grad, out_grad = final_sums(
+        *exchange("share_sums", 6, ("za2a", qkv_term), ("za2a", ysum), ("ya2a", zsum))
     )
-    return (jnp.sum(qkv_pieces, 0), jnp.sum(out_pieces, 0).T)
+    return qkv_grad, out_grad.T
 
 
 def solution(mesh):

time: 248 us -> 200 us (0.81)
  the two profiles are of different devices: /device:TPU:2 before, /device:TPU:4 now
where the time goes in v3:
time: 200 us; the launch traced here: 198 us
  Pallas kernels  185 us (92%)
  other arithmetic  6.21 us (3%)
  local copies, waits for them, and re-layouts  5.11 us (3%)
    pallas_call x6, Pallas kernels, exchange(): pl.pallas_call(functools.partial(comm_kernel, kinds), out_shape=shapes, i...  167 us
    pallas_call x1, Pallas kernels, attend_back(): pl.pallas_call(back_kernel, out_shape=jax.ShapeDtypeStruct((rows, 3 * HD)...  7.06 us
    pallas_call x1, Pallas kernels, attend(): pl.pallas_call(attend_kernel, out_shape=(jax.ShapeDtypeStruct((rows, HD),...  5.19 us

profile of v3, /device:TPU:4, one launch (start us, length us, event | category | flops | bytes accessed | tf_op | source)
XLA Modules:
  0.0 198.2 jit_solution(15423551127677699776)
XLA Ops:
  0.6 0.0 copy-start
  0.6 0.0 copy-start.4
  0.7 0.9 dynamic_slice.7
  1.6 0.0 copy-start.5
  1.6 0.0 copy-start.1
  1.6 2.2 %convert_reduce_fusion = f32[384]{0:T(512)S(1)} fusion(bf16[384,3072]{1,0:T(8,128)(2,1)} %param.8), kind=kLoop, calls=%fused_computation.1 | loop fusion | flops 2358912 | bytes 2360832 | tf_op jit(solution)/shard_map/reduce_sum | solution.py:618
  3.8 0.0 copy-done.4
  3.8 0.0 copy-start.6
  3.8 0.8 fusion.2
  4.6 0.0 copy-done.5
  4.6 0.1 copy.21.gate_ref
  4.7 1.8 constant_dynamic-slice_fusion
  6.5 1.1 copy.24
  7.6 0.0 copy-done.1
  7.6 1.2 copy.18
  8.8 0.0 copy-done.6
  8.8 2.8 %fusion.5.refs_1_ = bf16[384,3072]{1,0:T(8,128)(2,1)S(1)} fusion(bf16[384,3072]{1,0:T(8,128)(2,1)} %param.8, f32[3072]{0:T(1024)S(1)} %copy-done.6, f32[3072]{0:T(1024)S(1)} %broadcast_add_fusion, f32[384]{0:T(512)S(1)} %add_rsqrt_fusion.2, f32[384]{0:T(512)S(1)} %broadcast_multiply_fusion), kind=kLoop, calls=%fused_computation.7 | loop fusion | flops 7077888 | bytes 4746240 | tf_op jit(solution)/shard_map/convert_element_type | solution.py:620
  11.6 0.0 copy-done
  11.6 0.0 copy-start.2
  11.6 1.4 fusion.6.proj_ref
  13.0 0.0 copy-start.3
  13.0 0.2 multiply_reduce_fusion
  13.3 0.2 multiply_convert_fusion
  13.5 0.0 copy-done.2
  13.5 39.2 %share_kv.1 = (bf16[16,384,256]{2,1,0:T(8,128)(2,1)S(1)}, bf16[16,192,128]{2,1,0:T(8,128)(2,1)S(1)}) custom-call(bf16[384,256]{1,0:T(8,128)(2,1)S(1)} %pad_maximum_fusion.refs_0_, bf16[16,192,128]{2,1,0:T(8,128)(2,1)S(1)} %bitcast.8), custom_call_target="tpu_custom_call" | custom-call | tf_op jit(solution)/shard_map/share_kv/pallas_call | solution.py:324
  52.7 0.0 copy-done.3
  52.7 5.2 %attend.1 = (bf16[384,128]{1,0:T(8,128)(2,1)S(1)}, f32[384,128]{1,0:T(8,128)S(1)}) custom-call(s32[16]{0:T(128)S(1)} %copy-done.3, bf16[384,128]{1,0:T(8,128)(2,1)S(1)} %get-tuple-element.56.query_ref.refs_1_, bf16[16,384,256]{2,1,0:T(8,128)(2,1)S(1)} %get-tuple-element.29.kv_ref), custom_call_target="tpu_custom_call" | custom-call | tf_op jit(solution)/shard_map/attend/pallas_call | solution.py:379
  57.9 26.1 %share_att.1 = (bf16[16,384,128]{2,1,0:T(8,128)(2,1)S(1)}, bf16[16,384,128]{2,1,0:T(8,128)(2,1)S(1)}) custom-call(bf16[384,128]{1,0:T(8,128)(2,1)S(1)} %get-tuple-element.30.refs_0_.att_ref, bf16[384,128]{1,0:T(8,128)(2,1)S(1)} %get-tuple-element.56.query_ref.refs_1_), custom_call_target="tpu_custom_call" | custom-call | tf_op jit(solution)/shard_map/share_att/pallas_call | solution.py:324
  84.1 0.9 branch_grad.1.refs_0_
  84.9 19.1 %share_grad.1 = (bf16[16,192,384]{2,1,0:T(8,128)(2,1)S(1)}, bf16[4,384,768]{2,1,0:T(8,128)(2,1)S(1)}) custom-call(bf16[192,384]{1,0:T(8,128)(2,1)S(1)} %branch_grad.1.refs_0_, bf16[384,3072]{1,0:T(8,128)(2,1)S(1)} %fusion.5.refs_1_), custom_call_target="tpu_custom_call" | custom-call | tf_op jit(solution)/shard_map/share_grad/pallas_call | solution.py:324
  104.1 1.5 out_grads.1
  105.6 23.1 %share_gatt.1 = (bf16[16,384,128]{2,1,0:T(8,128)(2,1)S(1)}, f32[16,8,384]{2,1,0:T(8,128)S(1)}) custom-call(bf16[384,128]{1,0:T(8,128)(2,1)S(1)} %get-tuple-element.36.refs_0_, f32[8,384]{1,0:T(8,128)S(1)} %get-tuple-element.37.refs_1_), custom_call_target="tpu_custom_call" | custom-call | tf_op jit(solution)/shard_map/share_gatt/pallas_call | solution.py:324
  128.7 7.1 %attend_back.1.refs_0_ = bf16[384,384]{1,0:T(8,128)(2,1)S(1)} custom-call(s32[16]{0:T(128)S(1)} %copy-done.3, f32[384,384]{1,0:T(8,128)S(1)} %fusion.6.proj_ref, bf16[16,384,128]{2,1,0:T(8,128)(2,1)S(1)} %get-tuple-element.33.query_ref, bf16[16,384,256]{2,1,0:T(8,128)(2,1)S(1)} %get-tuple-element.29.kv_ref, ...), custom_call_target="tpu_custom_call" | custom-call | tf_op jit(solution)/shard_map/attend_back/pallas_call | solution.py:541
  135.8 26.0 %share_qkv.1 = (bf16[4,384,384]{2,1,0:T(8,128)(2,1)S(1)}, f32[4,384,128]{2,1,0:T(8,128)S(1)}, f32[4,384,128]{2,1,0:T(8,128)S(1)}) custom-call(bf16[384,384]{1,0:T(8,128)(2,1)S(1)} %attend_back.1.refs_0_, f32[4,384,128]{2,1,0:T(8,128)S(1)} %get-tuple-element.41.refs_1_, f32[4,384,128]{2,1,0:T(8,128)S(1)} %get-tuple-element.42.refs_2_), custom_call_target="tpu_custom_call" | custom-call | tf_op jit(solution)/shard_map/share_qkv/pallas_call | solution.py:324
  161.7 2.3 %grad_terms.1 = (f32[4,192,384]{2,1,0:T(8,128)S(1)}, f32[4,96,128]{2,1,0:T(8,128)S(1)}, f32[4,96,128]{2,1,0:T(8,128)S(1)}) custom-call(bf16[4,384,768]{2,1,0:T(8,128)(2,1)S(1)} %get-tuple-element.32.normed_ref, bf16[4,384,384]{2,1,0:T(8,128)(2,1)S(1)} %get-tuple-element.43.grad_ref, f32[4,384,128]{2,1,0:T(8,128)S(1)} %get-tuple-element.44.yparts_ref, ...), custom_call_target="tpu_custom_call" | custom-call | tf_op jit(solution)/shard_map/grad_terms/pallas_call | solution.py:578
  164.1 33.3 %share_sums.1 = (f32[4,192,384]{2,1,0:T(8,128)S(1)}, f32[4,96,128]{2,1,0:T(8,128)S(1)}, f32[4,96,128]{2,1,0:T(8,128)S(1)}) custom-call(f32[4,192,384]{2,1,0:T(8,128)S(1)} %get-tuple-element.46.refs_0_, f32[4,96,128]{2,1,0:T(8,128)S(1)} %get-tuple-element.47.refs_1_, f32[4,96,128]{2,1,0:T(8,128)S(1)} %get-tuple-element.48.refs_2_), custom_call_target="tpu_custom_call" | custom-call | tf_op jit(solution)/shard_map/share_sums/pallas_call | solution.py:324
  197.4 0.8 final_sums.1
  (6 shorter events, 0.1 us)
Async XLA Ops:
  0.6 11.0 %copy-start = (bf16[3072,384]{1,0:T(8,128)(2,1)S(1)}, bf16[3072,384]{1,0:T(8,128)(2,1)}, u32[]{:S(2)}) copy-start(bf16[3072,384]{1,0:T(8,128)(2,1)} %param.12) | copy-start | bytes 7077892
  0.6 3.2 %copy-start.4 = (bf16[384,3072]{1,0:T(8,128)(2,1)S(1)}, bf16[384,3072]{1,0:T(8,128)(2,1)}, u32[]{:S(2)}) copy-start(bf16[384,3072]{1,0:T(8,128)(2,1)} %param.8) | copy-start | bytes 7077892
  1.6 3.0 %copy-start.5 = (f32[3072]{0:T(1024)S(1)}, f32[3072]{0:T(1024)}, u32[]{:S(2)}) copy-start(f32[3072]{0:T(1024)} %param.10) | copy-start | bytes 36868
  1.6 6.0 %copy-start.1 = (bf16[128,3072]{1,0:T(8,128)(2,1)S(1)}, bf16[128,3072]{1,0:T(8,128)(2,1)}, u32[]{:S(2)}) copy-start(bf16[128,3072]{1,0:T(8,128)(2,1)} %weight_ref.1) | copy-start | bytes 2359300
  3.8 4.9 %copy-start.6 = (f32[3072]{0:T(1024)S(1)}, f32[3072]{0:T(1024)}, u32[]{:S(2)}) copy-start(f32[3072]{0:T(1024)} %param.9) | copy-start | bytes 36868
  11.6 1.9 copy-start.2
  13.0 39.7 %copy-start.3 = (s32[16]{0:T(128)S(1)}, s32[16]{0:T(128)}, u32[]{:S(2)}) copy-start(s32[16]{0:T(128)} %slots_ref.3) | copy-start | bytes 196

commit v4 on v3

--- a/solution.py
+++ b/solution.py
@@ -47,7 +47,7 @@
         return lax.rem(self.x + j, 4) * 4 + lo
 
 
-TASK_SEMS = {"tag": 20, "hag": 18, "ha2a": 16, "ycols": 8, "yag": 5, "ya2a": 4, "za2a": 4}
+TASK_SEMS = {"tag": 20, "hag": 18, "ha2a": 16, "ycols": 8, "yag": 5, "yrs": 6, "zrs": 6}
 
 
 def task_peers(kind):
@@ -57,23 +57,26 @@
         return {("h", j, 0) for j in (1, 3)} | {("h", 0, 2), ("h", 0, 1)}
     if kind == "ha2a":
         return {("h", j, f) for j in range(4) for f in range(4)} - {("h", 0, 0)}
-    if kind == "za2a":
-        return {("t", 0, k) for k in (1, 2, 3)}
-    if kind == "yag":
+    if kind == "zrs":
+        return {("t", 0, k) for k in (1, 3)}
+    if kind in ("yag", "yrs"):
         return {("t", j, 0) for j in (1, 3)}
     if kind == "ycols":
         return {("t", j, 0) for j in (1, 2, 3)} | {("h", 0, 1)}
-    return {("t", j, 0) for j in (1, 2, 3)}
+    raise ValueError(kind)
 
 
 def out_slots(kind):
+    if kind in ("yrs", "zrs"):
+        return 3
     return 16 if kind in ("tag", "hag", "ha2a") else 4
 
 
 def comm_kernel(kinds, *refs):
     n = len(kinds)
     ins, outs = refs[:n], refs[n : 2 * n]
-    sems = refs[2 * n :]
+    sems = refs[2 * n : 5 * n]
+    holds = list(refs[5 * n :])
     at = Places()
 
     def device(peer):
@@ -276,7 +279,8 @@
             steps.append((999, share))
             steps.append((1002, finish))
         else:
-            along_z = kind == "za2a"
+            along_z = kind == "zrs"
+            held, summed = holds.pop(0), holds.pop(0)
 
             def spot(j, along_z=along_z):
                 return lax.rem((at.b if along_z else at.a) + j, SIDE)
@@ -284,14 +288,30 @@
             def peer_of(j, along_z=along_z):
                 return ("t", 0, j) if along_z else ("t", j, 0)
 
-            for j in (1, 3, 2):
-                send(i, src.at[spot(j)], out.at[spot(0)], j, peer_of(j))
-            keep(i, src.at[spot(0)], spot(0))
-
-            def finish(i=i, out=out, spot=spot, peer_of=peer_of):
-                for j in (1, 3, 2):
-                    arrive(i, out.at[spot(4 - j)], j, peer_of(j))
-
+            rows = src.shape[1] // 2
+            parts = (pl.ds(0, rows), pl.ds(rows, rows))
+            for part, j in ((0, 1), (1, 3)):
+                send(i, src.at[spot(2), parts[part]], held.at[part], part, peer_of(j))
+            for part, j in ((0, 1), (1, 3)):
+                rest = parts[1 - part]
+                send(i, src.at[spot(j), rest], out.at[1 + part, rest], 2 + part, peer_of(j))
+            keep(i, src.at[spot(0)], 0)
+
+            def add(
+                i=i, src=src, out=out, held=held, summed=summed, spot=spot, peer_of=peer_of, parts=parts
+            ):
+                for part, j in ((0, 1), (1, 3)):
+                    arrive(i, held.at[part], part, peer_of(j))
+                    summed[part] = src[spot(j), parts[part], :] + held[part]
+                for part, j in ((0, 1), (1, 3)):
+                    send(i, summed.at[part], out.at[1 + part, parts[part]], 4 + part, peer_of(j))
+
+            def finish(i=i, out=out, peer_of=peer_of, parts=parts):
+                for part, j in ((0, 1), (1, 3)):
+                    arrive(i, out.at[1 + part, parts[1 - part]], 2 + part, peer_of(j))
+                    arrive(i, out.at[1 + part, parts[part]], 4 + part, peer_of(j))
+
+            steps.append((2, add))
             steps.append((1000, finish))
 
     for _, step in sorted(steps, key=lambda step: step[0]):
@@ -321,6 +341,10 @@
             pltpu.SemaphoreType.DMA((TASK_SEMS[kind],)),
             pltpu.SemaphoreType.DMA((1,)),
         ]
+    for kind, array in tasks:
+        if kind in ("yrs", "zrs"):
+            piece = (2, array.shape[1] // 2) + array.shape[2:]
+            scratch += [pltpu.VMEM(piece, array.dtype)] * 2
     return pl.pallas_call(
         functools.partial(comm_kernel, kinds),
         out_shape=shapes,
@@ -567,9 +591,7 @@
         half = sum_ref.shape[1]
         for k in range(sum_ref.shape[0]):
             rows = slice(k * half, (k + 1) * half)
-            sum_ref[k] = (parts_ref[0, rows] + parts_ref[1, rows]) + (
-                parts_ref[2, rows] + parts_ref[3, rows]
-            )
+            sum_ref[k] = parts_ref[0, rows] + (parts_ref[1, rows] + parts_ref[2, rows])
 
 
 def grad_terms(normed_parts, qkv_parts, yparts, zparts):
@@ -590,9 +612,9 @@
 
 
 def sums_kernel(qkv_ref, first_ref, second_ref, qkv_out_ref, out_out_ref):
-    qkv_out_ref[...] = (qkv_ref[0] + qkv_ref[1]) + (qkv_ref[2] + qkv_ref[3])
-    first = (first_ref[0] + first_ref[1]) + (first_ref[2] + first_ref[3])
-    second = (second_ref[0] + second_ref[1]) + (second_ref[2] + second_ref[3])
+    qkv_out_ref[...] = qkv_ref[0] + (qkv_ref[1] + qkv_ref[2])
+    first = first_ref[0] + (first_ref[1] + first_ref[2])
+    second = second_ref[0] + (second_ref[1] + second_ref[2])
     half = first.shape[0]
     out_out_ref[:half, :] = first
     out_out_ref[half:, :] = second
@@ -648,11 +670,11 @@
         slot_tiles, projected, all_query, all_kv, all_gatt, all_stats, inv, delta
     )
     qkv_parts, yparts, zparts = exchange(
-        "share_qkv", 5, ("yag", grad_qkv), ("ya2a", yterm), ("za2a", zterm)
+        "share_qkv", 5, ("yag", grad_qkv), ("yrs", yterm), ("zrs", zterm)
     )
     qkv_term, ysum, zsum = grad_terms(normed_parts, qkv_parts, yparts, zparts)
     qkv_grad, out_grad = final_sums(
-        *exchange("share_sums", 6, ("za2a", qkv_term), ("za2a", ysum), ("ya2a", zsum))
+        *exchange("share_sums", 6, ("zrs", qkv_term), ("zrs", ysum), ("yrs", zsum))
     )
     return qkv_grad, out_grad.T
 

time: 200 us -> 187 us (0.935)
  Pallas kernels: 185 us -> 171 us
    pallas_call x6, Pallas kernels: 167 us -> 153 us  [exchange(): pl.pallas_call(functools.partial(comm_kernel, kinds), out_shape=shapes, i...]
where the time goes in v4:
time: 187 us; the launch traced here: 184 us
  Pallas kernels  171 us (91%)
  other arithmetic  6.21 us (3%)
  local copies, waits for them, and re-layouts  5.11 us (3%)
    pallas_call x6, Pallas kernels, exchange(): pl.pallas_call(functools.partial(comm_kernel, kinds), out_shape=shapes, i...  153 us
    pallas_call x1, Pallas kernels, attend_back(): pl.pallas_call(back_kernel, out_shape=jax.ShapeDtypeStruct((rows, 3 * HD)...  7.03 us
    pallas_call x1, Pallas kernels, attend(): pl.pallas_call(attend_kernel, out_shape=(jax.ShapeDtypeStruct((rows, HD),...  5.22 us

profile of v4, /device:TPU:4, one launch (start us, length us, event | category | flops | bytes accessed | tf_op | source)
XLA Modules:
  0.0 184.5 jit_solution(11970927053423057304)
XLA Ops:
  0.6 0.0 copy-start
  0.6 0.0 copy-start.4
  0.7 0.9 dynamic_slice.7
  1.6 0.0 copy-start.5
  1.6 0.0 copy-start.1
  1.6 2.2 %convert_reduce_fusion = f32[384]{0:T(512)S(1)} fusion(bf16[384,3072]{1,0:T(8,128)(2,1)} %param.8), kind=kLoop, calls=%fused_computation.1 | loop fusion | flops 2358912 | bytes 2360832 | tf_op jit(solution)/shard_map/reduce_sum | solution.py:640
  3.8 0.0 copy-done.4
  3.8 0.0 copy-start.6
  3.8 0.8 fusion.2
  4.6 0.0 copy-done.5
  4.6 0.1 copy.21.gate_ref
  4.7 1.8 constant_dynamic-slice_fusion
  6.5 1.1 copy.24
  7.6 0.0 copy-done.1
  7.6 1.2 copy.18
  8.8 0.0 copy-done.6
  8.8 2.8 %fusion.5.refs_1_ = bf16[384,3072]{1,0:T(8,128)(2,1)S(1)} fusion(bf16[384,3072]{1,0:T(8,128)(2,1)} %param.8, f32[3072]{0:T(1024)S(1)} %copy-done.6, f32[3072]{0:T(1024)S(1)} %broadcast_add_fusion, f32[384]{0:T(512)S(1)} %add_rsqrt_fusion.2, f32[384]{0:T(512)S(1)} %broadcast_multiply_fusion), kind=kLoop, calls=%fused_computation.7 | loop fusion | flops 7077888 | bytes 4746240 | tf_op jit(solution)/shard_map/convert_element_type | solution.py:642
  11.6 0.0 copy-done
  11.6 0.0 copy-start.2
  11.6 1.4 fusion.6.proj_ref
  13.0 0.0 copy-start.3
  13.0 0.2 multiply_reduce_fusion
  13.3 0.2 multiply_convert_fusion
  13.5 0.0 copy-done.2
  13.5 39.2 %share_kv.1 = (bf16[16,384,256]{2,1,0:T(8,128)(2,1)S(1)}, bf16[16,192,128]{2,1,0:T(8,128)(2,1)S(1)}) custom-call(bf16[384,256]{1,0:T(8,128)(2,1)S(1)} %pad_maximum_fusion.refs_0_, bf16[16,192,128]{2,1,0:T(8,128)(2,1)S(1)} %bitcast.8), custom_call_target="tpu_custom_call" | custom-call | tf_op jit(solution)/shard_map/share_kv/pallas_call | solution.py:348
  52.7 0.0 copy-done.3
  52.7 5.2 %attend.1 = (bf16[384,128]{1,0:T(8,128)(2,1)S(1)}, f32[384,128]{1,0:T(8,128)S(1)}) custom-call(s32[16]{0:T(128)S(1)} %copy-done.3, bf16[384,128]{1,0:T(8,128)(2,1)S(1)} %get-tuple-element.56.query_ref.refs_1_, bf16[16,384,256]{2,1,0:T(8,128)(2,1)S(1)} %get-tuple-element.29.kv_ref), custom_call_target="tpu_custom_call" | custom-call | tf_op jit(solution)/shard_map/attend/pallas_call | solution.py:403
  58.0 24.4 %share_att.1 = (bf16[16,384,128]{2,1,0:T(8,128)(2,1)S(1)}, bf16[16,384,128]{2,1,0:T(8,128)(2,1)S(1)}) custom-call(bf16[384,128]{1,0:T(8,128)(2,1)S(1)} %get-tuple-element.30.refs_0_.att_ref, bf16[384,128]{1,0:T(8,128)(2,1)S(1)} %get-tuple-element.56.query_ref.refs_1_), custom_call_target="tpu_custom_call" | custom-call | tf_op jit(solution)/shard_map/share_att/pallas_call | solution.py:348
  82.4 0.9 branch_grad.1.refs_0_
  83.3 19.2 %share_grad.1 = (bf16[16,192,384]{2,1,0:T(8,128)(2,1)S(1)}, bf16[4,384,768]{2,1,0:T(8,128)(2,1)S(1)}) custom-call(bf16[192,384]{1,0:T(8,128)(2,1)S(1)} %branch_grad.1.refs_0_, bf16[384,3072]{1,0:T(8,128)(2,1)S(1)} %fusion.5.refs_1_), custom_call_target="tpu_custom_call" | custom-call | tf_op jit(solution)/shard_map/share_grad/pallas_call | solution.py:348
  102.5 1.5 out_grads.1
  104.0 23.8 %share_gatt.1 = (bf16[16,384,128]{2,1,0:T(8,128)(2,1)S(1)}, f32[16,8,384]{2,1,0:T(8,128)S(1)}) custom-call(bf16[384,128]{1,0:T(8,128)(2,1)S(1)} %get-tuple-element.36.refs_0_, f32[8,384]{1,0:T(8,128)S(1)} %get-tuple-element.37.refs_1_), custom_call_target="tpu_custom_call" | custom-call | tf_op jit(solution)/shard_map/share_gatt/pallas_call | solution.py:348
  127.8 7.0 %attend_back.1.refs_0_ = bf16[384,384]{1,0:T(8,128)(2,1)S(1)} custom-call(s32[16]{0:T(128)S(1)} %copy-done.3, f32[384,384]{1,0:T(8,128)S(1)} %fusion.6.proj_ref, bf16[16,384,128]{2,1,0:T(8,128)(2,1)S(1)} %get-tuple-element.33.query_ref, bf16[16,384,256]{2,1,0:T(8,128)(2,1)S(1)} %get-tuple-element.29.kv_ref, ...), custom_call_target="tpu_custom_call" | custom-call | tf_op jit(solution)/shard_map/attend_back/pallas_call | solution.py:565
  134.8 20.6 %share_qkv.1 = (bf16[4,384,384]{2,1,0:T(8,128)(2,1)S(1)}, f32[3,384,128]{2,1,0:T(8,128)S(1)}, f32[3,384,128]{2,1,0:T(8,128)S(1)}) custom-call(bf16[384,384]{1,0:T(8,128)(2,1)S(1)} %attend_back.1.refs_0_, f32[4,384,128]{2,1,0:T(8,128)S(1)} %get-tuple-element.41.refs_1_, f32[4,384,128]{2,1,0:T(8,128)S(1)} %get-tuple-element.42.refs_2_), custom_call_target="tpu_custom_call" | custom-call | tf_op jit(solution)/shard_map/share_qkv/pallas_call | solution.py:348
  155.4 2.3 %grad_terms.1 = (f32[4,192,384]{2,1,0:T(8,128)S(1)}, f32[4,96,128]{2,1,0:T(8,128)S(1)}, f32[4,96,128]{2,1,0:T(8,128)S(1)}) custom-call(bf16[4,384,768]{2,1,0:T(8,128)(2,1)S(1)} %get-tuple-element.32.normed_ref, bf16[4,384,384]{2,1,0:T(8,128)(2,1)S(1)} %get-tuple-element.43.grad_ref, f32[3,384,128]{2,1,0:T(8,128)S(1)} %get-tuple-element.44.yparts_ref, ...), custom_call_target="tpu_custom_call" | custom-call | tf_op jit(solution)/shard_map/grad_terms/pallas_call | solution.py:600
  157.7 26.0 %share_sums.1 = (f32[3,192,384]{2,1,0:T(8,128)S(1)}, f32[3,96,128]{2,1,0:T(8,128)S(1)}, f32[3,96,128]{2,1,0:T(8,128)S(1)}) custom-call(f32[4,192,384]{2,1,0:T(8,128)S(1)} %get-tuple-element.46.refs_0_, f32[4,96,128]{2,1,0:T(8,128)S(1)} %get-tuple-element.47.refs_1_, f32[4,96,128]{2,1,0:T(8,128)S(1)} %get-tuple-element.48.refs_2_), custom_call_target="tpu_custom_call" | custom-call | tf_op jit(solution)/shard_map/share_sums/pallas_call | solution.py:348
  183.7 0.8 final_sums.1
  (6 shorter events, 0.1 us)
Async XLA Ops:
  0.6 11.0 %copy-start = (bf16[3072,384]{1,0:T(8,128)(2,1)S(1)}, bf16[3072,384]{1,0:T(8,128)(2,1)}, u32[]{:S(2)}) copy-start(bf16[3072,384]{1,0:T(8,128)(2,1)} %param.12) | copy-start | bytes 7077892
  0.6 3.2 %copy-start.4 = (bf16[384,3072]{1,0:T(8,128)(2,1)S(1)}, bf16[384,3072]{1,0:T(8,128)(2,1)}, u32[]{:S(2)}) copy-start(bf16[384,3072]{1,0:T(8,128)(2,1)} %param.8) | copy-start | bytes 7077892
  1.6 3.0 %copy-start.5 = (f32[3072]{0:T(1024)S(1)}, f32[3072]{0:T(1024)}, u32[]{:S(2)}) copy-start(f32[3072]{0:T(1024)} %param.10) | copy-start | bytes 36868
  1.6 6.0 %copy-start.1 = (bf16[128,3072]{1,0:T(8,128)(2,1)S(1)}, bf16[128,3072]{1,0:T(8,128)(2,1)}, u32[]{:S(2)}) copy-start(bf16[128,3072]{1,0:T(8,128)(2,1)} %weight_ref.1) | copy-start | bytes 2359300
  3.8 4.9 %copy-start.6 = (f32[3072]{0:T(1024)S(1)}, f32[3072]{0:T(1024)}, u32[]{:S(2)}) copy-start(f32[3072]{0:T(1024)} %param.9) | copy-start | bytes 36868
  11.6 1.9 %copy-start.2 = (bf16[3072,128]{1,0:T(8,128)(2,1)S(1)}, bf16[3072,128]{1,0:T(8,128)(2,1)}, u32[]{:S(2)}) copy-start(bf16[3072,128]{1,0:T(8,128)(2,1)} %copy.18) | copy-start | bytes 2359300
  13.0 39.7 %copy-start.3 = (s32[16]{0:T(128)S(1)}, s32[16]{0:T(128)}, u32[]{:S(2)}) copy-start(s32[16]{0:T(128)} %slots_ref.3) | copy-start | bytes 196

commit v5 on v4

--- a/solution.py
+++ b/solution.py
@@ -47,7 +47,7 @@
         return lax.rem(self.x + j, 4) * 4 + lo
 
 
-TASK_SEMS = {"tag": 20, "hag": 18, "ha2a": 16, "ycols": 8, "yag": 5, "yrs": 6, "zrs": 6}
+TASK_SEMS = {"tag": 30, "hag": 22, "ha2a": 16, "ycols": 8, "yag": 25, "yrs": 6, "zrs": 6}
 
 
 def task_peers(kind):
@@ -142,19 +142,40 @@
                     return at.tile(j, k)
                 return lax.rem(at.a + j, SIDE)
 
-            def spread(i, k, block, axis=axis, slot_of=slot_of, out=out):
+            def own(part, src=src):
+                rows = src.shape[0] // 2
+                if rows < 8:
+                    return src.at[:, pl.ds(*((0, 256), (256, src.shape[1] - 256))[part])]
+                return src.at[pl.ds(part * rows, rows)]
+
+            rest = 18 if kind == "hag" else 20
+            gap = 2 if kind == "hag" else 4
+
+            def spread(
+                i, k, block=None, axis=axis, slot_of=slot_of, half=half, rest=rest, gap=gap
+            ):
                 slot = slot_of(0, 4 - k if axis == "t" and k else k)
-                for j in (1, 3):
-                    send(i, block, out.at[slot], 4 * j + k, (axis, j, 0))
-
-            def relay(i, k, axis=axis, slot_of=slot_of, half=half, out=out, kind=kind):
+                for late in (0, 1):
+                    for j, first in ((1, 0), (3, 1)):
+                        part = first ^ late
+                        piece = half(slot, part) if block is None else block(part)
+                        index = rest + gap * first + k if late else 4 * j + k
+                        send(i, piece, half(slot, part), index, (axis, j, 0))
+
+            def relay(i, k, axis=axis, slot_of=slot_of, half=half):
+                back = 4 - k if axis == "t" and k else k
+                for j, part in ((1, 0), (3, 1)):
+                    piece = half(slot_of(4 - j, back), part)
+                    arrive(i, piece, 4 * j + k, (axis, j, 0))
+                    send(i, piece, piece, (8 + k, k)[part], (axis, j, 0))
+
+            def settle(i, k, axis=axis, slot_of=slot_of, half=half, out=out, rest=rest, gap=gap, kind=kind):
                 back = 4 - k if axis == "t" and k else k
                 for j, part in ((1, 0), (3, 1)):
                     slot = slot_of(4 - j, back)
-                    arrive(i, out.at[slot], 4 * j + k, (axis, j, 0))
-                    send(i, half(slot, part), half(slot, part), (8 + k, k)[part], (axis, j, 0))
+                    arrive(i, half(slot, 1 - part), rest + gap * part + k, (axis, j, 0))
                     if kind == "hag":
-                        send(i, out.at[slot], out.at[slot], (4 * j + 2 + k), ("h", 0, 1))
+                        send(i, out.at[slot], out.at[slot], 4 * j + 2 + k, ("h", 0, 1))
 
             def far(i, k, axis=axis, slot_of=slot_of, half=half, out=out, kind=kind):
                 back = 4 - k if axis == "t" and k else k
@@ -165,24 +186,28 @@
                     send(i, out.at[slot], out.at[slot], 10 + k, ("h", 0, 1))
 
             if kind == "tag":
-                for k in (1, 3):
-                    send(i, src, out.at[at.t], 16 + k, ("t", 0, k))
-                spread(i, 0, src)
+                for late in (0, 1):
+                    for k, first in ((1, 0), (3, 1)):
+                        part = first ^ late
+                        index = 28 + first if late else 16 + k
+                        send(i, own(part), half(at.t, part), index, ("t", 0, k))
+                spread(i, 0, own)
                 keep(i, src, at.t)
 
-                def onward(i=i, out=out, spread=spread, half=half):
+                def onward(i=i, spread=spread, half=half):
                     for k, part in ((1, 0), (3, 1)):
-                        slot = at.tile(0, 4 - k)
-                        arrive(i, out.at[slot], 16 + k, ("t", 0, k))
-                        piece = half(slot, part)
+                        piece = half(at.tile(0, 4 - k), part)
+                        arrive(i, piece, 16 + k, ("t", 0, k))
                         send(i, piece, piece, (16, 18)[part], ("t", 0, k))
-                        spread(i, k, out.at[slot])
+                    for k, part in ((1, 0), (3, 1)):
+                        arrive(i, half(at.tile(0, 4 - k), 1 - part), 28 + part, ("t", 0, k))
+                        spread(i, k)
 
                 def last(i=i, out=out, spread=spread, half=half):
                     slot = at.tile(0, 2)
                     arrive(i, half(slot, 0), 16, ("t", 0, 1))
                     arrive(i, half(slot, 1), 18, ("t", 0, 3))
-                    spread(i, 2, out.at[slot])
+                    spread(i, 2)
 
                 steps.append((2, functools.partial(relay, i, 0)))
                 steps.append((3, onward))
@@ -191,17 +216,18 @@
                 steps.append((5.5, functools.partial(relay, i, 3)))
                 steps.append((7, functools.partial(relay, i, 2)))
                 for k in (0, 1, 3, 2):
+                    steps.append((1000, functools.partial(settle, i, k)))
                     steps.append((1000, functools.partial(far, i, k)))
             elif kind == "hag":
                 send(i, src, out.at[at.h], 16, ("h", 0, 2))
-                spread(i, 0, src)
+                spread(i, 0, own)
                 send(i, src, out.at[at.h], 2, ("h", 0, 1))
                 keep(i, src, at.h)
 
                 def onward(i=i, out=out, spread=spread):
                     slot = at.head(0, 2)
                     arrive(i, out.at[slot], 16, ("h", 0, 2))
-                    spread(i, 1, out.at[slot])
+                    spread(i, 1)
                     send(i, out.at[slot], out.at[slot], 3, ("h", 0, 1))
 
                 def finish(i=i, out=out):
@@ -212,28 +238,18 @@
 
                 steps.append((1, onward))
                 steps.append((1.5, functools.partial(relay, i, 0)))
+                steps.append((1.6, functools.partial(settle, i, 0)))
                 steps.append((3.2, functools.partial(relay, i, 1)))
+                steps.append((4.5, functools.partial(settle, i, 1)))
                 steps.append((4, functools.partial(far, i, 0)))
                 steps.append((5.2, functools.partial(far, i, 1)))
                 steps.append((1001, finish))
             else:
-                for j in (1, 3):
-                    send(i, src, out.at[at.a], j, ("t", j, 0))
+                spread(i, 0, own)
                 keep(i, src, at.a)
-
-                def pass_on(i=i, half=half, out=out):
-                    for j, part in ((1, 0), (3, 1)):
-                        slot = lax.rem(at.a + 4 - j, SIDE)
-                        arrive(i, out.at[slot], j, ("t", j, 0))
-                        send(i, half(slot, part), half(slot, part), (2, 4)[part], ("t", j, 0))
-
-                def finish(i=i, half=half):
-                    slot = lax.rem(at.a + 2, SIDE)
-                    arrive(i, half(slot, 0), 2, ("t", 1, 0))
-                    arrive(i, half(slot, 1), 4, ("t", 3, 0))
-
-                steps.append((1, pass_on))
-                steps.append((1000, finish))
+                steps.append((1, functools.partial(relay, i, 0)))
+                steps.append((1000, functools.partial(settle, i, 0)))
+                steps.append((1000, functools.partial(far, i, 0)))
         elif kind == "ha2a":
             def give(i=i, src=src, out=out, flips=()):
                 for f in flips:

time: 187 us -> 186 us (level)
    pallas_call x6, Pallas kernels: 153 us -> 157 us  [exchange(): pl.pallas_call(functools.partial(comm_kernel, kinds), out_shape=shapes, i...]
where the time goes in v5:
time: 186 us; the launch traced here: 185 us
  Pallas kernels  171 us (92%)
  other arithmetic  6.21 us (3%)
  local copies, waits for them, and re-layouts  5.11 us (3%)
    pallas_call x6, Pallas kernels, exchange(): pl.pallas_call(functools.partial(comm_kernel, kinds), out_shape=shapes, i...  157 us
    pallas_call x1, Pallas kernels, attend_back(): pl.pallas_call(back_kernel, out_shape=jax.ShapeDtypeStruct((rows, 3 * HD)...  5.22 us
    pallas_call x1, Pallas kernels, attend(): pl.pallas_call(attend_kernel, out_shape=(jax.ShapeDtypeStruct((rows, HD),...  4.05 us

profile of v5, /device:TPU:4, one launch (start us, length us, event | category | flops | bytes accessed | tf_op | source)
XLA Modules:
  0.0 184.9 jit_solution(5926889283210062807)
XLA Ops:
  0.6 0.0 copy-start
  0.6 0.0 copy-start.4
  0.7 0.9 dynamic_slice.7
  1.6 0.0 copy-start.5
  1.6 0.0 copy-start.1
  1.6 2.2 %convert_reduce_fusion = f32[384]{0:T(512)S(1)} fusion(bf16[384,3072]{1,0:T(8,128)(2,1)} %param.8), kind=kLoop, calls=%fused_computation.1 | loop fusion | flops 2358912 | bytes 2360832 | tf_op jit(solution)/shard_map/reduce_sum | solution.py:656
  3.8 0.0 copy-done.4
  3.8 0.0 copy-start.6
  3.8 0.8 fusion.2
  4.6 0.0 copy-done.5
  4.6 0.1 copy.21.gate_ref
  4.7 1.8 constant_dynamic-slice_fusion
  6.5 1.1 copy.24
  7.6 0.0 copy-done.1
  7.6 1.2 copy.18
  8.8 0.0 copy-done.6
  8.8 2.8 %fusion.5.refs_1_ = bf16[384,3072]{1,0:T(8,128)(2,1)S(1)} fusion(bf16[384,3072]{1,0:T(8,128)(2,1)} %param.8, f32[3072]{0:T(1024)S(1)} %copy-done.6, f32[3072]{0:T(1024)S(1)} %broadcast_add_fusion, f32[384]{0:T(512)S(1)} %add_rsqrt_fusion.2, f32[384]{0:T(512)S(1)} %broadcast_multiply_fusion), kind=kLoop, calls=%fused_computation.7 | loop fusion | flops 7077888 | bytes 4746240 | tf_op jit(solution)/shard_map/convert_element_type | solution.py:658
  11.6 0.0 copy-done
  11.6 0.0 copy-start.2
  11.6 1.4 fusion.6.proj_ref
  13.0 0.0 copy-start.3
  13.0 0.2 multiply_reduce_fusion
  13.3 0.2 multiply_convert_fusion
  13.5 0.0 copy-done.2
  13.5 39.3 %share_kv.1 = (bf16[16,384,256]{2,1,0:T(8,128)(2,1)S(1)}, bf16[16,192,128]{2,1,0:T(8,128)(2,1)S(1)}) custom-call(bf16[384,256]{1,0:T(8,128)(2,1)S(1)} %pad_maximum_fusion.refs_0_, bf16[16,192,128]{2,1,0:T(8,128)(2,1)S(1)} %bitcast.8), custom_call_target="tpu_custom_call" | custom-call | tf_op jit(solution)/shard_map/share_kv/pallas_call | solution.py:364
  52.8 0.0 copy-done.3
  52.8 4.1 %attend.1 = (bf16[384,128]{1,0:T(8,128)(2,1)S(1)}, f32[384,128]{1,0:T(8,128)S(1)}) custom-call(s32[16]{0:T(128)S(1)} %copy-done.3, bf16[384,128]{1,0:T(8,128)(2,1)S(1)} %get-tuple-element.56.query_ref.refs_1_, bf16[16,384,256]{2,1,0:T(8,128)(2,1)S(1)} %get-tuple-element.29.kv_ref), custom_call_target="tpu_custom_call" | custom-call | tf_op jit(solution)/shard_map/attend/pallas_call | solution.py:419
  56.8 27.5 %share_att.1 = (bf16[16,384,128]{2,1,0:T(8,128)(2,1)S(1)}, bf16[16,384,128]{2,1,0:T(8,128)(2,1)S(1)}) custom-call(bf16[384,128]{1,0:T(8,128)(2,1)S(1)} %get-tuple-element.30.refs_0_.att_ref, bf16[384,128]{1,0:T(8,128)(2,1)S(1)} %get-tuple-element.56.query_ref.refs_1_), custom_call_target="tpu_custom_call" | custom-call | tf_op jit(solution)/shard_map/share_att/pallas_call | solution.py:364
  84.4 0.9 branch_grad.1.refs_0_
  85.2 18.2 %share_grad.1 = (bf16[16,192,384]{2,1,0:T(8,128)(2,1)S(1)}, bf16[4,384,768]{2,1,0:T(8,128)(2,1)S(1)}) custom-call(bf16[192,384]{1,0:T(8,128)(2,1)S(1)} %branch_grad.1.refs_0_, bf16[384,3072]{1,0:T(8,128)(2,1)S(1)} %fusion.5.refs_1_), custom_call_target="tpu_custom_call" | custom-call | tf_op jit(solution)/shard_map/share_grad/pallas_call | solution.py:364
  103.5 1.5 out_grads.1
  105.0 24.7 %share_gatt.1 = (bf16[16,384,128]{2,1,0:T(8,128)(2,1)S(1)}, f32[16,8,384]{2,1,0:T(8,128)S(1)}) custom-call(bf16[384,128]{1,0:T(8,128)(2,1)S(1)} %get-tuple-element.36.refs_0_, f32[8,384]{1,0:T(8,128)S(1)} %get-tuple-element.37.refs_1_), custom_call_target="tpu_custom_call" | custom-call | tf_op jit(solution)/shard_map/share_gatt/pallas_call | solution.py:364
  129.6 5.2 %attend_back.1.refs_0_ = bf16[384,384]{1,0:T(8,128)(2,1)S(1)} custom-call(s32[16]{0:T(128)S(1)} %copy-done.3, f32[384,384]{1,0:T(8,128)S(1)} %fusion.6.proj_ref, bf16[16,384,128]{2,1,0:T(8,128)(2,1)S(1)} %get-tuple-element.33.query_ref, bf16[16,384,256]{2,1,0:T(8,128)(2,1)S(1)} %get-tuple-element.29.kv_ref, ...), custom_call_target="tpu_custom_call" | custom-call | tf_op jit(solution)/shard_map/attend_back/pallas_call | solution.py:581
  134.9 22.3 %share_qkv.1 = (bf16[4,384,384]{2,1,0:T(8,128)(2,1)S(1)}, f32[3,384,128]{2,1,0:T(8,128)S(1)}, f32[3,384,128]{2,1,0:T(8,128)S(1)}) custom-call(bf16[384,384]{1,0:T(8,128)(2,1)S(1)} %attend_back.1.refs_0_, f32[4,384,128]{2,1,0:T(8,128)S(1)} %get-tuple-element.41.refs_1_, f32[4,384,128]{2,1,0:T(8,128)S(1)} %get-tuple-element.42.refs_2_), custom_call_target="tpu_custom_call" | custom-call | tf_op jit(solution)/shard_map/share_qkv/pallas_call | solution.py:364
  157.1 2.3 %grad_terms.1 = (f32[4,192,384]{2,1,0:T(8,128)S(1)}, f32[4,96,128]{2,1,0:T(8,128)S(1)}, f32[4,96,128]{2,1,0:T(8,128)S(1)}) custom-call(bf16[4,384,768]{2,1,0:T(8,128)(2,1)S(1)} %get-tuple-element.32.normed_ref, bf16[4,384,384]{2,1,0:T(8,128)(2,1)S(1)} %get-tuple-element.43.grad_ref, f32[3,384,128]{2,1,0:T(8,128)S(1)} %get-tuple-element.44.yparts_ref, ...), custom_call_target="tpu_custom_call" | custom-call | tf_op jit(solution)/shard_map/grad_terms/pallas_call | solution.py:616
  159.5 24.6 %share_sums.1 = (f32[3,192,384]{2,1,0:T(8,128)S(1)}, f32[3,96,128]{2,1,0:T(8,128)S(1)}, f32[3,96,128]{2,1,0:T(8,128)S(1)}) custom-call(f32[4,192,384]{2,1,0:T(8,128)S(1)} %get-tuple-element.46.refs_0_, f32[4,96,128]{2,1,0:T(8,128)S(1)} %get-tuple-element.47.refs_1_, f32[4,96,128]{2,1,0:T(8,128)S(1)} %get-tuple-element.48.refs_2_), custom_call_target="tpu_custom_call" | custom-call | tf_op jit(solution)/shard_map/share_sums/pallas_call | solution.py:364
  184.1 0.8 final_sums.1
  (6 shorter events, 0.1 us)
Async XLA Ops:
  0.6 11.0 %copy-start = (bf16[3072,384]{1,0:T(8,128)(2,1)S(1)}, bf16[3072,384]{1,0:T(8,128)(2,1)}, u32[]{:S(2)}) copy-start(bf16[3072,384]{1,0:T(8,128)(2,1)} %param.12) | copy-start | bytes 7077892
  0.6 3.2 %copy-start.4 = (bf16[384,3072]{1,0:T(8,128)(2,1)S(1)}, bf16[384,3072]{1,0:T(8,128)(2,1)}, u32[]{:S(2)}) copy-start(bf16[384,3072]{1,0:T(8,128)(2,1)} %param.8) | copy-start | bytes 7077892
  1.6 3.0 %copy-start.5 = (f32[3072]{0:T(1024)S(1)}, f32[3072]{0:T(1024)}, u32[]{:S(2)}) copy-start(f32[3072]{0:T(1024)} %param.10) | copy-start | bytes 36868
  1.6 6.0 %copy-start.1 = (bf16[128,3072]{1,0:T(8,128)(2,1)S(1)}, bf16[128,3072]{1,0:T(8,128)(2,1)}, u32[]{:S(2)}) copy-start(bf16[128,3072]{1,0:T(8,128)(2,1)} %weight_ref.1) | copy-start | bytes 2359300
  3.8 4.9 %copy-start.6 = (f32[3072]{0:T(1024)S(1)}, f32[3072]{0:T(1024)}, u32[]{:S(2)}) copy-start(f32[3072]{0:T(1024)} %param.9) | copy-start | bytes 36868
  11.6 1.9 %copy-start.2 = (bf16[3072,128]{1,0:T(8,128)(2,1)S(1)}, bf16[3072,128]{1,0:T(8,128)(2,1)}, u32[]{:S(2)}) copy-start(bf16[3072,128]{1,0:T(8,128)(2,1)} %copy.18) | copy-start | bytes 2359300
  13.0 39.7 %copy-start.3 = (s32[16]{0:T(128)S(1)}, s32[16]{0:T(128)}, u32[]{:S(2)}) copy-start(s32[16]{0:T(128)} %slots_ref.3) | copy-start | bytes 196

commit v6 on v5

--- a/solution.py
+++ b/solution.py
@@ -257,7 +257,7 @@
                         if f or j:
                             send(i, src.at[at.head(j, f)], out.at[at.h], 4 * f + j, ("h", j, f))
 
-            give(flips=(1, 0))
+            steps.append((3.3, functools.partial(give, flips=(1, 0))))
             keep(i, src.at[at.h], at.h)
             steps.append((5, functools.partial(give, flips=(3, 2))))
 
@@ -675,9 +675,11 @@
     teacher_part = lax.dynamic_slice_in_dim(teacher, head * step, step, 1).T
     gate_part = lax.dynamic_slice_in_dim(mod_gate, head * step, step, 0)[:, None]
 
-    all_kv, weight_parts = exchange("share_kv", 1, ("tag", kv), ("ha2a", weight_t))
+    (all_kv,) = exchange("share_kv", 1, ("tag", kv))
     attended, inv = attend(slot_tiles, query_b, all_kv)
-    att_parts, all_query = exchange("share_att", 2, ("hag", attended), ("tag", query_b))
+    att_parts, all_query, weight_parts = exchange(
+        "share_att", 2, ("hag", attended), ("tag", query_b), ("ha2a", weight_t)
+    )
     grad_part = branch_grad(weight_parts, att_parts, teacher_part, gate_part)
     grad_parts, normed_parts = exchange("share_grad", 3, ("hag", grad_part), ("ycols", normed))
     yterm, zterm, gatt, stats, delta = out_grads(grad_parts, out_weight, attended, inv)

time: 186 us -> 189 us (1.016)
  Pallas kernels: 171 us -> 174 us
    pallas_call x6, Pallas kernels: 157 us -> 152 us  [exchange(): pl.pallas_call(functools.partial(comm_kernel, kinds), out_shape=shapes, i...]
    pallas_call x1, Pallas kernels: 5.22 us -> 9.79 us  [attend_back(): pl.pallas_call(back_kernel, out_shape=jax.ShapeDtypeStruct((rows, 3 * HD)...]
    pallas_call x1, Pallas kernels: 4.05 us -> 6.92 us  [attend(): pl.pallas_call(attend_kernel, out_shape=(jax.ShapeDtypeStruct((rows, HD),...]
where the time goes in v6:
time: 189 us; the launch traced here: 187 us
  Pallas kernels  174 us (92%)
  other arithmetic  6.2 us (3%)
  local copies, waits for them, and re-layouts  5.1 us (3%)
    pallas_call x6, Pallas kernels, exchange(): pl.pallas_call(functools.partial(comm_kernel, kinds), out_shape=shapes, i...  152 us
    pallas_call x1, Pallas kernels, attend_back(): pl.pallas_call(back_kernel, out_shape=jax.ShapeDtypeStruct((rows, 3 * HD)...  9.79 us
    pallas_call x1, Pallas kernels, attend(): pl.pallas_call(attend_kernel, out_shape=(jax.ShapeDtypeStruct((rows, HD),...  6.92 us

profile of v6, /device:TPU:4, one launch (start us, length us, event | category | flops | bytes accessed | tf_op | source)
XLA Modules:
  0.0 187.3 jit_solution(12633013060661173540)
XLA Ops:
  0.6 0.0 copy-start
  0.6 0.0 copy-start.4
  0.7 0.9 dynamic_slice.7
  1.6 0.0 copy-start.5
  1.6 0.0 copy-start.1
  1.6 2.2 %convert_reduce_fusion = f32[384]{0:T(512)S(1)} fusion(bf16[384,3072]{1,0:T(8,128)(2,1)} %param.8), kind=kLoop, calls=%fused_computation.1 | loop fusion | flops 2358912 | bytes 2360832 | tf_op jit(solution)/shard_map/reduce_sum | solution.py:656
  3.8 0.0 copy-done.4
  3.8 0.0 copy-start.6
  3.8 0.8 fusion.2
  4.6 0.0 copy-done.5
  4.6 0.1 copy.21.gate_ref
  4.7 1.8 constant_dynamic-slice_fusion
  6.5 1.1 copy.24
  7.6 0.0 copy-done.1
  7.6 1.2 copy.19
  8.8 0.0 copy-done.6
  8.8 2.8 %fusion.5.refs_1_ = bf16[384,3072]{1,0:T(8,128)(2,1)S(1)} fusion(bf16[384,3072]{1,0:T(8,128)(2,1)} %param.8, f32[3072]{0:T(1024)S(1)} %copy-done.6, f32[3072]{0:T(1024)S(1)} %broadcast_add_fusion, f32[384]{0:T(512)S(1)} %add_rsqrt_fusion.2, f32[384]{0:T(512)S(1)} %broadcast_multiply_fusion), kind=kLoop, calls=%fused_computation.7 | loop fusion | flops 7077888 | bytes 4746240 | tf_op jit(solution)/shard_map/convert_element_type | solution.py:658
  11.6 0.0 copy-done
  11.6 1.4 fusion.6.proj_ref
  13.0 0.2 multiply_reduce_fusion
  13.2 0.0 copy-start.3
  13.3 0.2 multiply_convert_fusion
  13.5 37.6 %share_kv.1.kv_ref = bf16[16,384,256]{2,1,0:T(8,128)(2,1)S(1)} custom-call(bf16[384,256]{1,0:T(8,128)(2,1)S(1)} %pad_maximum_fusion.refs_0_), custom_call_target="tpu_custom_call" | custom-call | tf_op jit(solution)/shard_map/share_kv/pallas_call | solution.py:364
  51.1 0.0 copy-done.3
  51.1 0.0 copy-start.2
  51.1 6.9 %attend.1 = (bf16[384,128]{1,0:T(8,128)(2,1)S(1)}, f32[384,128]{1,0:T(8,128)S(1)}) custom-call(s32[16]{0:T(128)S(1)} %copy-done.3, bf16[384,128]{1,0:T(8,128)(2,1)S(1)} %get-tuple-element.55.query_ref.refs_1_, bf16[16,384,256]{2,1,0:T(8,128)(2,1)S(1)} %share_kv.1.kv_ref), custom_call_target="tpu_custom_call" | custom-call | tf_op jit(solution)/shard_map/attend/pallas_call | solution.py:419
  58.0 0.0 copy-done.2
  58.0 29.1 %share_att.1 = (bf16[16,384,128]{2,1,0:T(8,128)(2,1)S(1)}, bf16[16,384,128]{2,1,0:T(8,128)(2,1)S(1)}, bf16[16,192,128]{2,1,0:T(8,128)(2,1)S(1)}) custom-call(bf16[384,128]{1,0:T(8,128)(2,1)S(1)} %get-tuple-element.27.refs_0_.att_ref, bf16[384,128]{1,0:T(8,128)(2,1)S(1)} %get-tuple-element.55.query_ref.refs_1_, bf16[16,192,128]{2,1,0:T(8,128)(2,1)S(1)} %bitcast.8), custom_call_target="tpu_custom_call" | custom-call | tf_op jit(solution)/shard_map/share_att/pallas_call | solution.py:364
  87.1 0.9 branch_grad.1.refs_0_
  88.0 18.3 %share_grad.1 = (bf16[16,192,384]{2,1,0:T(8,128)(2,1)S(1)}, bf16[4,384,768]{2,1,0:T(8,128)(2,1)S(1)}) custom-call(bf16[192,384]{1,0:T(8,128)(2,1)S(1)} %branch_grad.1.refs_0_, bf16[384,3072]{1,0:T(8,128)(2,1)S(1)} %fusion.5.refs_1_), custom_call_target="tpu_custom_call" | custom-call | tf_op jit(solution)/shard_map/share_grad/pallas_call | solution.py:364
  106.3 1.5 out_grads.1
  107.8 23.5 %share_gatt.1 = (bf16[16,384,128]{2,1,0:T(8,128)(2,1)S(1)}, f32[16,8,384]{2,1,0:T(8,128)S(1)}) custom-call(bf16[384,128]{1,0:T(8,128)(2,1)S(1)} %get-tuple-element.34.refs_0_, f32[8,384]{1,0:T(8,128)S(1)} %get-tuple-element.35.refs_1_), custom_call_target="tpu_custom_call" | custom-call | tf_op jit(solution)/shard_map/share_gatt/pallas_call | solution.py:364
  131.4 9.8 %attend_back.1.refs_0_ = bf16[384,384]{1,0:T(8,128)(2,1)S(1)} custom-call(s32[16]{0:T(128)S(1)} %copy-done.3, f32[384,384]{1,0:T(8,128)S(1)} %fusion.6.proj_ref, bf16[16,384,128]{2,1,0:T(8,128)(2,1)S(1)} %get-tuple-element.31.query_ref, bf16[16,384,256]{2,1,0:T(8,128)(2,1)S(1)} %share_kv.1.kv_ref, bf16[16,384,128]{2,1,0:T(8,128)(2,1)S(1)} %get-tuple-element.36.gatt_ref, ...), custom_call_target="tpu_custom_call" | custom-call | tf_op jit(solution)/shard_map/attend_back/pallas_call | solution.py:581
  141.2 18.4 %share_qkv.1 = (bf16[4,384,384]{2,1,0:T(8,128)(2,1)S(1)}, f32[3,384,128]{2,1,0:T(8,128)S(1)}, f32[3,384,128]{2,1,0:T(8,128)S(1)}) custom-call(bf16[384,384]{1,0:T(8,128)(2,1)S(1)} %attend_back.1.refs_0_, f32[4,384,128]{2,1,0:T(8,128)S(1)} %get-tuple-element.39.refs_1_, f32[4,384,128]{2,1,0:T(8,128)S(1)} %get-tuple-element.40.refs_2_), custom_call_target="tpu_custom_call" | custom-call | tf_op jit(solution)/shard_map/share_qkv/pallas_call | solution.py:364
  159.6 2.3 %grad_terms.1 = (f32[4,192,384]{2,1,0:T(8,128)S(1)}, f32[4,96,128]{2,1,0:T(8,128)S(1)}, f32[4,96,128]{2,1,0:T(8,128)S(1)}) custom-call(bf16[4,384,768]{2,1,0:T(8,128)(2,1)S(1)} %get-tuple-element.30.normed_ref, bf16[4,384,384]{2,1,0:T(8,128)(2,1)S(1)} %get-tuple-element.41.grad_ref, f32[3,384,128]{2,1,0:T(8,128)S(1)} %get-tuple-element.42.yparts_ref, ...), custom_call_target="tpu_custom_call" | custom-call | tf_op jit(solution)/shard_map/grad_terms/pallas_call | solution.py:616
  162.0 24.5 %share_sums.1 = (f32[3,192,384]{2,1,0:T(8,128)S(1)}, f32[3,96,128]{2,1,0:T(8,128)S(1)}, f32[3,96,128]{2,1,0:T(8,128)S(1)}) custom-call(f32[4,192,384]{2,1,0:T(8,128)S(1)} %get-tuple-element.44.refs_0_, f32[4,96,128]{2,1,0:T(8,128)S(1)} %get-tuple-element.45.refs_1_, f32[4,96,128]{2,1,0:T(8,128)S(1)} %get-tuple-element.46.refs_2_), custom_call_target="tpu_custom_call" | custom-call | tf_op jit(solution)/shard_map/share_sums/pallas_call | solution.py:364
  186.5 0.8 final_sums.1
  (6 shorter events, 0.1 us)
Async XLA Ops:
  0.6 11.0 %copy-start = (bf16[3072,384]{1,0:T(8,128)(2,1)S(1)}, bf16[3072,384]{1,0:T(8,128)(2,1)}, u32[]{:S(2)}) copy-start(bf16[3072,384]{1,0:T(8,128)(2,1)} %param.12) | copy-start | bytes 7077892
  0.6 3.2 %copy-start.4 = (bf16[384,3072]{1,0:T(8,128)(2,1)S(1)}, bf16[384,3072]{1,0:T(8,128)(2,1)}, u32[]{:S(2)}) copy-start(bf16[384,3072]{1,0:T(8,128)(2,1)} %param.8) | copy-start | bytes 7077892
  1.6 3.0 %copy-start.5 = (f32[3072]{0:T(1024)S(1)}, f32[3072]{0:T(1024)}, u32[]{:S(2)}) copy-start(f32[3072]{0:T(1024)} %param.10) | copy-start | bytes 36868
  1.6 6.0 %copy-start.1 = (bf16[128,3072]{1,0:T(8,128)(2,1)S(1)}, bf16[128,3072]{1,0:T(8,128)(2,1)}, u32[]{:S(2)}) copy-start(bf16[128,3072]{1,0:T(8,128)(2,1)} %weight_ref.1) | copy-start | bytes 2359300
  3.8 4.9 %copy-start.6 = (f32[3072]{0:T(1024)S(1)}, f32[3072]{0:T(1024)}, u32[]{:S(2)}) copy-start(f32[3072]{0:T(1024)} %param.9) | copy-start | bytes 36868
  13.2 37.9 %copy-start.3 = (s32[16]{0:T(128)S(1)}, s32[16]{0:T(128)}, u32[]{:S(2)}) copy-start(s32[16]{0:T(128)} %slots_ref.3) | copy-start | bytes 196
  51.1 6.9 %copy-start.2 = (bf16[3072,128]{1,0:T(8,128)(2,1)S(1)}, bf16[3072,128]{1,0:T(8,128)(2,1)}, u32[]{:S(2)}) copy-start(bf16[3072,128]{1,0:T(8,128)(2,1)} %copy.19) | copy-start | bytes 2359300
